TPU v7x, 32 devices: a whole 2x2x4 slice. The times are simulated.
32 devices in a mesh: tile: 8 (over z, y), depth: 4 (over x, core).
Axes of the slice: x: 2, y: 2, z: 4, core: 2. Of those that a mesh axis runs over, the one named last changes fastest.
Arguments:
- positions: float32 [3, 16384], P(None, 'tile'), may hold values from -4 to 4
- log_scales: float32 [3, 16384], P(None, 'tile'), may hold values from -2 to 0
- opacity_logits: float32 [1, 16384], P(None, 'tile'), may hold values from -3 to 1.5
- colors: float32 [3, 16384], P(None, 'tile'), may hold values from 0 to 1
- first_moment: float32 [10, 16384], P(None, 'tile'), may hold values from -3 to 3
- second_moment: float32 [10, 16384], P(None, 'tile'), may hold values from 0.01 to 1
- cameras: float32 [4, 2, 4], replicated, may hold values from -6.4 to 6.4
- background: float32 [3], replicated, may hold values from 0 to 1
- target: float32 [32, 3, 1024], P('tile'), may hold values from 0 to 1
- tile_view: int32 [32], P('tile'), may hold values from 0 to 3
- tile_length: int32 [32], P('tile'), may hold values from 128 to 512
- list_owner: int32 [4, 32, 128, 1], P('depth', 'tile'), may hold values from 0 to 7; in each aligned block of 512 rows (0 to 511, 512 to 1023, ..., all dimensions but the last counted through in order) at most 160 rows name the same one
- list_row: int32 [4, 32, 128], P('depth', 'tile'), may hold values from 0 to 2047
Outputs:
- image: float32 [32, 3, 1024], P('tile')
- new_params: float32 [10, 16384], P(None, 'tile')
- new_first: float32 [10, 16384], P(None, 'tile')
- new_second: float32 [10, 16384], P(None, 'tile')
Inputs may be any that keep to these rules, and one draw needn't show every extreme that they name: `list_owner`: within the entries of one device's block (one depth slab of the tiles of one tile index), no owner is named more than 160 times, a bound that some block reaches.
All inputs are finite; a program needn't handle non-finite values.
Results may differ from a plain program's by a relative error of at most 0.00008.
Values sent between devices are 32-bit elements; how exact they have to be, the bound alone decides.
A program may use at most 64 MiB of HBM per device.

v0:
```python
import jax
import jax.numpy as jnp
from jax import lax
from jax.sharding import PartitionSpec as P

TILE_SIDE = 32


def project(params, cams):
    position = params[0:3]
    variance = jnp.exp(2.0 * params[3:6])
    first_row = cams[:, 0, 0:3].T
    second_row = cams[:, 1, 0:3].T
    center_x = jnp.sum(first_row * position, axis=0) + cams[:, 0, 3] + 0.5 * TILE_SIDE
    center_y = jnp.sum(second_row * position, axis=0) + cams[:, 1, 3] + 0.5 * TILE_SIDE
    cov_xx = jnp.sum(first_row * first_row * variance, axis=0) + 0.3
    cov_xy = jnp.sum(first_row * second_row * variance, axis=0)
    cov_yy = jnp.sum(second_row * second_row * variance, axis=0) + 0.3
    determinant = cov_xx * cov_yy - cov_xy * cov_xy
    return jnp.stack(
        [
            center_x,
            center_y,
            cov_yy / determinant,
            -cov_xy / determinant,
            cov_xx / determinant,
            jax.nn.sigmoid(params[6]),
            params[7],
            params[8],
            params[9],
        ]
    )


def coverage(screen, alive, pixels):
    pixel = jnp.arange(pixels, dtype=jnp.int32)
    pixel_x = (pixel % TILE_SIDE).astype(jnp.float32) + 0.5
    pixel_y = (pixel // TILE_SIDE).astype(jnp.float32) + 0.5
    offset_x = pixel_x[:, None] - screen[0][None, :]
    offset_y = pixel_y[:, None] - screen[1][None, :]
    quadric = (
        screen[2][None, :] * offset_x * offset_x
        + 2.0 * screen[3][None, :] * offset_x * offset_y
        + screen[4][None, :] * offset_y * offset_y
    )
    falloff = jnp.exp(-0.5 * quadric)
    alpha = screen[5][None, :] * falloff * alive[None, :]
    return (offset_x, offset_y, falloff, alpha)


def running_sum(values, triangle):
    rows = values.shape[0]
    width = triangle.shape[0]
    blocks = values.reshape(rows, values.shape[1] // width, width)
    inner = jnp.einsum("pbk,kj->pbj", blocks, triangle, precision=lax.Precision.HIGHEST)
    sums = jnp.sum(blocks, axis=2)
    lead = jnp.cumsum(sums, axis=1) - sums
    return (inner + lead[:, :, None]).reshape(rows, values.shape[1])


def adam_update(param, first, second, gradient):
    new_first = 0.9 * first + 0.1 * gradient
    new_second = 0.999 * second + 0.001 * gradient * gradient
    corrected = new_first / (1.0 - 0.9**10) / (jnp.sqrt(new_second / (1.0 - 0.999**10)) + 1e-08)
    return (param - 0.05 * corrected, new_first, new_second)


def body(
    positions,
    log_scales,
    opacity_logits,
    colors,
    first_moment,
    second_moment,
    cameras,
    background,
    target,
    tile_view,
    tile_length,
    list_owner,
    list_row,
):
    tiles_here = target.shape[0]
    pixels = target.shape[2]
    slab = list_row.shape[2]
    owner_count = lax.axis_size("tile")
    depth_count = lax.axis_size("depth")
    depth_index = lax.axis_index("depth")
    capacity = max(2, 5 * tiles_here * slab // (2 * owner_count))
    highest = lax.Precision.HIGHEST
    params = jnp.concatenate([positions, log_scales, opacity_logits, colors], axis=0)
    owner = list_owner.reshape(-1)
    wanted = list_row.reshape(-1)
    viewed = jnp.repeat(tile_view, slab)
    onehot = (owner[:, None] == jnp.arange(owner_count, dtype=jnp.int32)[None, :]).astype(jnp.int32)
    rank = jnp.sum((jnp.cumsum(onehot, axis=0) - onehot) * onehot, axis=1)
    slot = owner * capacity + rank
    request = (
        jnp.zeros((2, owner_count * capacity), jnp.int32)
        .at[:, slot]
        .set(jnp.stack([wanted, viewed]))
    )
    request = request.reshape(2, owner_count, capacity)
    received = lax.all_to_all(request, "tile", split_axis=1, concat_axis=1, tiled=True)
    rows_in = received[0].reshape(-1)
    views_in = received[1].reshape(-1)
    screen = project(params[:, rows_in], cameras[views_in])
    screen = screen.reshape(9, received.shape[1], received.shape[2])
    fetched = lax.all_to_all(screen, "tile", split_axis=1, concat_axis=1, tiled=True)
    entry = fetched.reshape(9, -1)[:, slot].reshape(9, tiles_here, slab).transpose(1, 0, 2)
    order = jnp.arange(slab, dtype=jnp.int32)
    strict = (order[:, None] < order[None, :]).astype(jnp.float32)
    inclusive = (order[:, None] <= order[None, :]).astype(jnp.float32)

    def forward(args):
        screen, alive = args
        offset_x, offset_y, falloff, alpha = coverage(screen, alive, pixels)
        leak = jnp.log1p(-alpha)
        before = running_sum(leak, strict)
        weight = alpha * jnp.exp(before)
        color = jnp.einsum("ck,pk->cp", screen[6:9], weight, precision=highest)
        return (jnp.sum(leak, axis=1), color)

    def backward(args):
        screen, alive, start_log, start_color, whole, miss = args
        offset_x, offset_y, falloff, alpha = coverage(screen, alive, pixels)
        leak = jnp.log1p(-alpha)
        local = running_sum(leak, strict)
        carried = jnp.exp(start_log)[:, None]
        inside = jnp.exp(local)
        trans = carried * inside
        weight = alpha * trans
        local_weight = alpha * inside
        d_alpha = jnp.zeros_like(alpha)
        for channel in range(3):
            shade = screen[6 + channel][None, :]
            upto = running_sum(local_weight * shade, inclusive)
            behind = whole[channel][:, None] - start_color[channel][:, None] - carried * upto
            d_alpha = d_alpha + miss[channel][:, None] * (trans * shade - behind / (1.0 - alpha))
        d_color = jnp.einsum("cp,pk->ck", miss, weight, precision=highest)
        d_quad = d_alpha * (-0.5 * alpha)
        d_opacity = jnp.sum(d_alpha * falloff * alive[None, :], axis=0)
        d_center_x = jnp.sum(
            d_quad * -2.0 * (screen[2][None, :] * offset_x + screen[3][None, :] * offset_y), axis=0
        )
        d_center_y = jnp.sum(
            d_quad * -2.0 * (screen[3][None, :] * offset_x + screen[4][None, :] * offset_y), axis=0
        )
        d_conic_a = jnp.sum(d_quad * offset_x * offset_x, axis=0)
        d_conic_b = jnp.sum(d_quad * 2.0 * offset_x * offset_y, axis=0)
        d_conic_c = jnp.sum(d_quad * offset_y * offset_y, axis=0)
        return jnp.concatenate(
            [
                jnp.stack([d_center_x, d_center_y, d_conic_a, d_conic_b, d_conic_c, d_opacity]),
                d_color,
            ],
            axis=0,
        )

    quarter = tiles_here // depth_count
    whole_entry = lax.all_to_all(entry, "depth", split_axis=0, concat_axis=2, tiled=True)
    first_tile = depth_index * quarter
    own_length = lax.dynamic_slice_in_dim(tile_length, first_tile, quarter, 0)
    full_place = jnp.arange(slab * depth_count, dtype=jnp.int32)
    own_live = (full_place[None, :] < own_length[:, None]).astype(jnp.float32)
    own_log, own_color = lax.map(forward, (whole_entry, own_live))
    own_image = own_color + jnp.exp(own_log)[:, None, :] * background[None, :, None]
    own_error = own_image - lax.dynamic_slice_in_dim(target, first_tile, quarter, 0)
    zero_log = jnp.zeros_like(own_log)
    zero_color = jnp.zeros_like(own_color)
    own_grad = lax.map(
        backward, (whole_entry, own_live, zero_log, zero_color, own_image, own_error)
    )
    entry_grad = lax.all_to_all(own_grad, "depth", split_axis=2, concat_axis=0, tiled=True)
    image = lax.all_gather(own_image, "depth", axis=0, tiled=True)
    flat_grad = entry_grad.transpose(1, 0, 2).reshape(9, -1)
    outgoing = jnp.zeros((9, owner_count * capacity), jnp.float32).at[:, slot].set(flat_grad)
    outgoing = outgoing.reshape(9, owner_count, capacity)
    incoming = lax.all_to_all(outgoing, "tile", split_axis=1, concat_axis=1, tiled=True)
    rows_in = received[0].reshape(-1)
    views_in = received[1].reshape(-1)
    chosen_cams = cameras[views_in]
    unused, pullback = jax.vjp(lambda chosen: project(chosen, chosen_cams), params[:, rows_in])
    (slot_grad,) = pullback(incoming.reshape(9, -1))
    gradient = jnp.zeros_like(params).at[:, rows_in].add(slot_grad)
    gradient = lax.psum(gradient, "depth")
    new_params, new_first, new_second = adam_update(params, first_moment, second_moment, gradient)
    return (image, new_params, new_first, new_second)


def solution(mesh):
    placed = (
        P(None, "tile"),
        P(None, "tile"),
        P(None, "tile"),
        P(None, "tile"),
        P(None, "tile"),
        P(None, "tile"),
        P(),
        P(),
        P("tile", None, None),
        P("tile"),
        P("tile"),
        P("depth", "tile", None, None),
        P("depth", "tile", None),
    )
    return jax.shard_map(
        body,
        mesh=mesh,
        in_specs=placed,
        out_specs=(P("tile", None, None), P(None, "tile"), P(None, "tile"), P(None, "tile")),
        check_vma=False,
    )
```

profile of v0, /device:TPU:0, one launch (start us, length us, event | category | flops | bytes accessed | tf_op | source)
XLA Modules:
  0.0 199.3 jit_solution(7363935695881023951)
XLA Ops:
  12.3 1.9 scatter_custom_fusion
  15.2 7.3 %all-to-all-start = ((s32[2,8,160]{2,0,1:T(2,128)}), s32[2,8,160]{2,0,1:T(2,128)S(1)}, u32[]{:S(2)}, u32[]{:S(2)}) async-start(s32[2,8,160]{2,0,1:T(2,128)} %copy.152), calls=%async_computation | async-start | bytes 32768 | tf_op jit(solution)/shard_map/all_to_all | solution.py:104
  24.3 4.7 %all-to-all-done = s32[2,8,160]{2,0,1:T(2,128)S(1)} async-done(((s32[2,8,160]{2,0,1:T(2,128)}), s32[2,8,160]{2,0,1:T(2,128)S(1)}, u32[]{:S(2)}, u32[]{:S(2)}) %all-to-all-start) | async-done | bytes 10272 | tf_op jit(solution)/shard_map/all_to_all | solution.py:104
  29.2 4.3 %gather_fusion = f32[1280,2,4]{2,1,0:T(2,128)S(1)} fusion(f32[4,2,4]{2,1,0:T(2,128)S(1)} %copy-done.1, s32[2048]{0:T(1024)S(1)} %pad_clamp_fusion.1), kind=kCustom, calls=%fused_computation | custom fusion | bytes 87040 | tf_op jit(solution)/shard_map/gather | solution.py:107
  35.3 36.3 %slice_reduce_fusion = (f32[1280]{0:T(1024)S(1)}, f32[1280]{0:T(1024)S(1)}) fusion(f32[1280,2,4]{2,1,0:T(2,128)S(1)} %gather_fusion), kind=kLoop, calls=%fused_computation.71 | loop fusion | bytes 20480 | tf_op jit(solution)/shard_map/slice | solution.py:15
  73.4 2.4 %gather_fusion.1 = f32[1280,10]{1,0:T(8,128)S(1)} fusion(f32[10,2048]{0,1:T(8,128)S(1)} %copy.154, s32[2048]{0:T(1024)S(1)} %pad_clamp_fusion), kind=kCustom, calls=%fused_computation.1 | custom fusion | bytes 107520 | tf_op jit(solution)/shard_map/gather | solution.py:107
  78.0 3.5 %all-to-all-start.1 = ((f32[8,1,1440]{2,1,0:T(1,128)}), f32[8,1,1440]{2,1,0:T(1,128)S(1)}, u32[]{:S(2)}, u32[]{:S(2)}) async-start(f32[8,1,1440]{2,1,0:T(1,128)} %reshape.1452), calls=%async_computation.1 | async-start | bytes 98304 | tf_op jit(solution)/shard_map/all_to_all | solution.py:109
  82.2 5.9 %all-to-all-done.1 = f32[8,1,1440]{2,1,0:T(1,128)S(1)} async-done(((f32[8,1,1440]{2,1,0:T(1,128)}), f32[8,1,1440]{2,1,0:T(1,128)S(1)}, u32[]{:S(2)}, u32[]{:S(2)}) %all-to-all-start.1) | async-done | bytes 46112 | tf_op jit(solution)/shard_map/all_to_all | solution.py:109
  91.5 3.3 %all-to-all-start.2 = ((f32[4,9,128]{2,1,0:T(8,128)}), f32[4,9,128]{2,1,0:T(8,128)S(1)}, u32[]{:S(2)}, u32[]{:S(2)}) async-start(f32[4,9,128]{2,1,0:T(8,128)} %bitcast.21), calls=%async_computation.2 | async-start | bytes 65536 | tf_op jit(solution)/shard_map/all_to_all | solution.py:161
  95.5 3.2 %all-to-all-done.2 = f32[4,9,128]{2,1,0:T(8,128)S(1)} async-done(((f32[4,9,128]{2,1,0:T(8,128)}), f32[4,9,128]{2,1,0:T(8,128)S(1)}, u32[]{:S(2)}, u32[]{:S(2)}) %all-to-all-start.2) | async-done | bytes 18464 | tf_op jit(solution)/shard_map/all_to_all | solution.py:161
  98.7 2.0 fusion.28
  100.8 5.9 %multiply_reduce_fusion.3 = (f32[1024,4]{0,1:T(4,128)S(1)}, f32[1024,4]{0,1:T(4,128)S(1)}, f32[1024,4]{0,1:T(4,128)S(1)}, f32[1024,4,128]{0,2,1:T(8,128)S(1)}, f32[1024,4,128]{0,2,1:T(8,128)}) fusion(f32[4,128]{1,0:T(4,128)S(1)} %bitcast.208, f32[4,128]{1,0:T(4,128)S(1)} %bitcast.188, f32[4,128]{1,0:T(4,128)S(1)} %bitcast.185, f32[1024,4]{0,1:T(4,128)S(1)} %sub.316, ...), kind=kOutput, calls=%fused_computation.60 | convolution fusion | flops 823660544 | bytes 4288512 | tf_op jit(solution)/shard_map/while/body/eval_jaxpr/pbk,kj->pbj/dot_general | solution.py:55
  106.7 2.9 %fusion.24 = f32[1024,4,128]{0,2,1:T(8,128)} fusion(f32[1024,4,128]{0,2,1:T(8,128)S(1)} %get-tuple-element.96, f32[4,128]{1,0:T(4,128)S(1)} %bitcast.189), kind=kOutput, calls=%fused_computation.58 | convolution fusion | flops 805847040 | bytes 4196352 | tf_op jit(solution)/shard_map/while/body/eval_jaxpr/pbk,kj->pbj/dot_general | solution.py:55
  109.6 2.9 %fusion.22 = f32[1024,4,128]{0,2,1:T(8,128)} fusion(f32[1024,4,128]{0,2,1:T(8,128)S(1)} %get-tuple-element.96, f32[4,128]{1,0:T(4,128)S(1)} %bitcast.186), kind=kOutput, calls=%fused_computation.55 | convolution fusion | flops 805847040 | bytes 4196352 | tf_op jit(solution)/shard_map/while/body/eval_jaxpr/pbk,kj->pbj/dot_general | solution.py:55
  112.5 1.9 fusion.14
  115.5 1.8 fusion.56
  117.5 6.2 %multiply_multiply_fusion = (f32[1024,4,128]{0,2,1:T(8,128)S(1)}, f32[1024,4,128]{0,2,1:T(8,128)S(1)}) fusion(f32[4,128]{1,0:T(4,128)S(1)} %fusion.74, f32[4,128]{1,0:T(4,128)S(1)} %bitcast.168, f32[4,128]{1,0:T(4,128)S(1)} %bitcast.173, f32[1024]{0:T(1024)S(1)} %get-tuple-element.136, f32[4,128]{1,0:T(4,128)S(1)} %broadcast_multiply_fusion.1, ...), kind=kOutput, calls=%fused_computation.49 | convolution fusion | flops 825245696 | bytes 12701696 | tf_op jit(solution)/shard_map/while/body/eval_jaxpr/pbk,kj->pbj/dot_general | solution.py:55
  123.7 3.8 %fusion.3 = (f32[4,128]{1,0:T(4,128)S(1)}, f32[4,128]{1,0:T(4,128)S(1)}, f32[4,128]{1,0:T(4,128)S(1)}, f32[4,128]{1,0:T(4,128)S(1)}, f32[4,128]{1,0:T(4,128)S(1)}, /*index=5*/f32[4,128]{1,0:T(4,128)S(1)}) fusion(f32[1024,4,128]{0,2,1:T(8,128)S(1)} %get-tuple-element.131, f32[4,128]{1,0:T(4,128)S(1)} %bitcast.162, f32[4,128]{1,0:T(4,128)S(1)} %bitcast.169, ...), kind=kLoop, calls=%fused_computation.29 | loop fusion | flops 17298432 | bytes 4229120 | tf_op jit(solution)/shard_map/while/body/eval_jaxpr/reduce_sum | solution.py:146
  129.4 6.2 %all_to_all.48 = f32[4,1,1152]{2,1,0:T(1,128)S(1)} all-to-all(f32[4,1,1152]{2,1,0:T(1,128)S(1)} %reshape.1454), channel_id=1, replica_groups=mesh['tile'=8,'depth'=4] {'depth'}, dimensions={0} | all-to-all | bytes 36864 | tf_op jit(solution)/shard_map/all_to_all | solution.py:174
  137.0 1.9 scatter_custom_fusion.1
  139.4 9.2 %all_to_all.49 = f32[8,1,1440]{2,1,0:T(1,128)S(1)} all-to-all(f32[8,1,1440]{2,1,0:T(1,128)S(1)} %reshape.1456), channel_id=1, replica_groups=mesh['tile'=8,'depth'=4] {'tile'}, dimensions={0} | all-to-all | bytes 92160 | tf_op jit(solution)/shard_map/all_to_all | solution.py:179
  150.8 10.3 %scatter_custom_fusion.2 = f32[10,2048]{0,1:T(8,128)S(1)} fusion(s32[1280]{0:T(1024)S(1)} %fusion.60, f32[1280,10]{1,0:T(8,128)S(1)} %copy.178, f32[]{:T(128)} %constant.132.clone.1), kind=kCustom, calls=%fused_computation.73 | custom fusion | flops 12800 | bytes 81924 | tf_op jit(solution)/shard_map/scatter-add | solution.py:185
  162.1 5.3 %all-gather.1 = f32[4,3,1024]{2,1,0:T(4,128)S(1)} all-gather(f32[1,3,1024]{2,1,0:T(4,128)S(1)} %get-tuple-element.130), channel_id=2, replica_groups=mesh['tile'=8,'depth'=4] {'depth'}, dimensions={0}, use_global_device_ids=true | all-gather | bytes 61440 | tf_op jit(solution)/shard_map/all_gather | solution.py:175
  168.1 22.6 %all-reduce.8.cloned.1.call-done = f32[10,2048]{1,0:T(8,128)} async-done(((f32[10,2048]{1,0:T(8,128)}), f32[10,2048]{1,0:T(8,128)}) %all-reduce.8.cloned.1.call-update) | async-done | bytes 81936 | tf_op jit(solution)/shard_map/psum | solution.py:186
  (127 shorter events, 29.1 us)
Async XLA Ops:
  7.2 15.3 %copy-start = (f32[4,3,1024]{2,0,1:T(4,128)S(1)}, f32[4,3,1024]{2,0,1:T(4,128)}, u32[]{:S(2)}) copy-start(f32[4,3,1024]{2,0,1:T(4,128)} %param.21) | copy-start | bytes 147460
  7.2 16.6 %copy-start.9 = (s32[4]{0:T(128)S(1)}, s32[4]{0:T(128)}, u32[]{:S(2)}) copy-start(s32[4]{0:T(128)} %param.23) | copy-start | bytes 52
  7.2 22.0 %copy-start.1 = (f32[4,2,4]{2,1,0:T(2,128)S(1)}, f32[4,2,4]{2,1,0:T(2,128)}, u32[]{:S(2)}) copy-start(f32[4,2,4]{2,1,0:T(2,128)} %param.19) | copy-start | bytes 388
  15.2 13.9 %all-to-all-start = ((s32[2,8,160]{2,0,1:T(2,128)}), s32[2,8,160]{2,0,1:T(2,128)S(1)}, u32[]{:S(2)}, u32[]{:S(2)}) async-start(s32[2,8,160]{2,0,1:T(2,128)} %copy.152), calls=%async_computation | async-start | bytes 32768 | tf_op jit(solution)/shard_map/all_to_all | solution.py:104
  78.0 10.1 %all-to-all-start.1 = ((f32[8,1,1440]{2,1,0:T(1,128)}), f32[8,1,1440]{2,1,0:T(1,128)S(1)}, u32[]{:S(2)}, u32[]{:S(2)}) async-start(f32[8,1,1440]{2,1,0:T(1,128)} %reshape.1452), calls=%async_computation.1 | async-start | bytes 98304 | tf_op jit(solution)/shard_map/all_to_all | solution.py:109
  91.5 7.2 %all-to-all-start.2 = ((f32[4,9,128]{2,1,0:T(8,128)}), f32[4,9,128]{2,1,0:T(8,128)S(1)}, u32[]{:S(2)}, u32[]{:S(2)}) async-start(f32[4,9,128]{2,1,0:T(8,128)} %bitcast.21), calls=%async_computation.2 | async-start | bytes 65536 | tf_op jit(solution)/shard_map/all_to_all | solution.py:161
  94.8 95.9 %all-reduce.8.cloned.1.call-start = ((), (), s32[]{:S(2)}) async-start(), calls=%async_computation.5 | async-start | bytes 262144 | tf_op jit(solution)/shard_map/psum | solution.py:186
  109.6 4.8 %copy-start.8 = (f32[3]{0:T(128)S(1)}, f32[3]{0:T(128)}, u32[]{:S(2)}) copy-start(f32[3]{0:T(128)} %param.20) | copy-start | bytes 40
  149.3 41.4 %copy-start.2 = (f32[3,2048]{1,0:T(4,128)S(1)}, f32[3,2048]{1,0:T(4,128)}, u32[]{:S(2)}) copy-start(f32[3,2048]{1,0:T(4,128)} %param.16) | copy-start | bytes 73732
  149.3 41.3 %copy-start.3 = (f32[3,2048]{1,0:T(4,128)S(1)}, f32[3,2048]{1,0:T(4,128)}, u32[]{:S(2)}) copy-start(f32[3,2048]{1,0:T(4,128)} %param.14) | copy-start | bytes 73732
  149.3 41.3 %copy-start.4 = (f32[3,2048]{1,0:T(4,128)S(1)}, f32[3,2048]{1,0:T(4,128)}, u32[]{:S(2)}) copy-start(f32[3,2048]{1,0:T(4,128)} %param.13) | copy-start | bytes 73732
  149.3 41.3 %copy-start.5 = (f32[10,2048]{1,0:T(8,128)S(1)}, f32[10,2048]{1,0:T(8,128)}, u32[]{:S(2)}) copy-start(f32[10,2048]{1,0:T(8,128)} %param.17) | copy-start | bytes 245764
  149.3 41.3 %copy-start.6 = (f32[10,2048]{1,0:T(8,128)S(1)}, f32[10,2048]{1,0:T(8,128)}, u32[]{:S(2)}) copy-start(f32[10,2048]{1,0:T(8,128)} %param.18) | copy-start | bytes 245764
  149.4 41.3 %copy-start.7 = (f32[1,2048]{1,0:T(1,128)S(1)}, f32[1,2048]{1,0:T(1,128)}, u32[]{:S(2)}) copy-start(f32[1,2048]{1,0:T(1,128)} %param.15) | copy-start | bytes 24580
Sparse Core Ops, SparseCore 0:
  162.2 28.3 all-reduce.7
where the time goes:
time: 200 us; the launch traced here: 199 us
  local copies, waits for them, and re-layouts  62.6 us (31%)
  waiting for transfers between devices  36.4 us (18%)
  other arithmetic  30.1 us (15%)
  matrix products  20.8 us (10%)
  blocking collectives  20.7 us (10%)
  between operations  14.6 us (7%)
  starting transfers between devices  14.1 us (7%)
    slice x1, local copies, waits for them, and re-layouts, project(): cams[:, 1, 3]  36.3 us
    psum x1, waiting for transfers between devices, body(): gradient = lax.psum(gradient, 'depth')  22.6 us
    dot_general x4, matrix products, running_sum(): jnp.einsum('pbk,kj->pbj', blocks, triangle, precision=lax.Precision.HIGHEST)  17.9 us
    scatter-add x1, other arithmetic, body(): gradient = jnp.zeros_like(params).at[:, rows_in].add(slot_grad)  10.3 us
    all_to_all x1, blocking collectives, body(): lax.all_to_all(outgoing, 'tile', split_axis=1, concat_axis=1, tiled=True)  9.17 us
    all_to_all x1, starting transfers between devices, body(): lax.all_to_all(request, 'tile', split_axis=1, concat_axis=1, tiled=True)  7.31 us
    gather x3, local copies, waits for them, and re-layouts, body(): screen = project(params[:, rows_in], cameras[views_in])  6.92 us
    all_to_all x1, blocking collectives, body(): lax.all_to_all(own_grad, 'depth', split_axis=2, concat_axis=0, tiled=True)  6.22 us
  transfers between devices with their start and end apart: 4, of which 4 were waited for; matrix products, arithmetic and copies ran while one was open for 2% of the time, Pallas kernels for 0%

commit v1 on v0

v1 whole, which is shorter than its diff:
```python
import functools

import jax
import jax.numpy as jnp
from jax import lax
from jax.experimental import pallas as pl
from jax.experimental.pallas import tpu as pltpu
from jax.sharding import PartitionSpec as P

TILE_SIDE = 32
LANES = 128
MESH = pl.DeviceIdType.MESH
F32 = jnp.float32
BF16 = jnp.bfloat16


def exchange(items, name, ident):
    axes = []
    for _, axis, _ in items:
        if axis not in axes:
            axes.append(axis)
    sizes = {axis: lax.axis_size(axis) for axis in axes}
    count = len(items)

    def kernel(*refs):
        sources, targets = refs[:count], refs[count : 2 * count]
        sems = refs[2 * count :]
        barrier = pltpu.get_barrier_semaphore()
        for axis in axes:
            me = lax.axis_index(axis)
            for step in range(1, sizes[axis]):
                peer = lax.rem(me + step, sizes[axis])
                pl.semaphore_signal(barrier, inc=1, device_id={axis: peer}, device_id_type=MESH)
        pl.semaphore_wait(barrier, sum(sizes[axis] - 1 for axis in axes))
        copies = []
        for place, (_, axis, mode) in enumerate(items):
            source, target = sources[place], targets[place]
            send, receive, own = sems[3 * place : 3 * place + 3]
            me = lax.axis_index(axis)
            size = sizes[axis]
            for step in range(size - 1, 0, -1):
                peer = lax.rem(me + step, size)
                copy = pltpu.make_async_remote_copy(
                    src_ref=source if mode == "gather" else source.at[peer],
                    dst_ref=target.at[me],
                    send_sem=send.at[step],
                    recv_sem=receive.at[step],
                    device_id={axis: peer},
                    device_id_type=MESH,
                )
                copy.start()
                copies.append(copy)
            local = pltpu.make_async_copy(
                source if mode == "gather" else source.at[me], target.at[me], own
            )
            local.start()
            copies.append(local)
        for copy in copies:
            copy.wait()

    outs = []
    scratch = []
    for array, axis, mode in items:
        size = sizes[axis]
        shape = (size,) + (array.shape if mode == "gather" else array.shape[1:])
        outs.append(jax.ShapeDtypeStruct(shape, array.dtype))
        scratch += [
            pltpu.SemaphoreType.DMA((size,)),
            pltpu.SemaphoreType.DMA((size,)),
            pltpu.SemaphoreType.DMA,
        ]
    space = pl.BlockSpec(memory_space=pltpu.VMEM)
    return pl.pallas_call(
        kernel,
        out_shape=outs,
        in_specs=[space] * count,
        out_specs=[space] * count,
        scratch_shapes=scratch,
        name=name,
        compiler_params=pltpu.CompilerParams(
            collective_id=ident, has_side_effects=True, vmem_limit_bytes=60 << 20
        ),
    )(*[array for array, _, _ in items])


def split3(x):
    high = x.astype(BF16)
    rest = x - high.astype(F32)
    middle = rest.astype(BF16)
    low = (rest - middle.astype(F32)).astype(BF16)
    return high, middle, low


def render_kernel(
    where_ref, view_ref, length_ref, cam_ref, back_ref,
    list_ref, param_ref, target_ref,
    image_ref, grad_ref,
    picked, alphas, transes, misses, columns, sums,
):
    owners, lines = param_ref.shape[0], param_ref.shape[1]
    slabs = list_ref.shape[0]
    entries = slabs * list_ref.shape[2]
    pixels = target_ref.shape[2]
    highs = lines // 10
    chunks = pixels // LANES
    groups = entries // 8
    tile = where_ref[0]
    length = length_ref[tile]
    view = view_ref[tile]

    owner = jnp.concatenate([list_ref[d, 0:1, :] for d in range(slabs)], axis=1)
    row = jnp.concatenate([list_ref[d, 1:2, :] for d in range(slabs)], axis=1)
    low_key = row & (LANES - 1)
    high_key = owner * highs + (row >> 7)
    onehot = jnp.where(
        lax.broadcasted_iota(jnp.int32, (LANES, entries), 0) == low_key, 1.0, 0.0
    ).astype(BF16)
    twice = jnp.concatenate([onehot, onehot], axis=0)
    high_iota = lax.broadcasted_iota(jnp.int32, (highs, entries), 0)
    picked[...] = jnp.zeros_like(picked)

    def gather(o, carry):
        high, middle, low = split3(param_ref[o])
        got = jnp.dot(
            jnp.concatenate([high, middle], axis=1), twice, preferred_element_type=F32
        ) + jnp.dot(low, onehot, preferred_element_type=F32)
        mask = high_iota == high_key - o * highs
        for p in range(10):
            part = pl.ds(p * highs, highs)
            picked[part, :] = jnp.where(mask, got[p * highs : (p + 1) * highs], picked[part, :])
        return carry

    lax.fori_loop(0, owners, gather, 0, unroll=min(owners, 4))
    values = [
        jnp.sum(picked[p * highs : (p + 1) * highs, :], axis=0, keepdims=True) for p in range(10)
    ]

    base = view * 8
    first = [cam_ref[base + j] for j in range(4)]
    second = [cam_ref[base + 4 + j] for j in range(4)]
    variance = [jnp.exp(2.0 * values[3 + j]) for j in range(3)]
    half = 0.5 * TILE_SIDE
    center_x = first[0] * values[0] + first[1] * values[1] + first[2] * values[2] + first[3] + half
    center_y = second[0] * values[0] + second[1] * values[1] + second[2] * values[2] + second[3] + half
    cov_xx = sum(first[j] * first[j] * variance[j] for j in range(3)) + 0.3
    cov_xy = sum(first[j] * second[j] * variance[j] for j in range(3))
    cov_yy = sum(second[j] * second[j] * variance[j] for j in range(3)) + 0.3
    determinant = cov_xx * cov_yy - cov_xy * cov_xy
    conic_a = cov_yy / determinant
    conic_b = -cov_xy / determinant
    conic_c = cov_xx / determinant
    opacity = 1.0 / (1.0 + jnp.exp(-values[6]))
    place = lax.broadcasted_iota(jnp.int32, (1, entries), 1)
    shown = jnp.where(place < length, opacity, 0.0)
    rows = [center_x, center_y, -0.5 * conic_a, -conic_b, -0.5 * conic_c, shown] + values[7:10]
    table = jnp.concatenate(rows + [jnp.zeros((LANES - len(rows), entries), F32)], axis=0)
    columns[...] = table.T

    lane = lax.broadcasted_iota(jnp.int32, (8, LANES), 1)
    sub = lax.broadcasted_iota(jnp.int32, (8, LANES), 0)
    pixel_x = (lane & (TILE_SIDE - 1)).astype(F32) + 0.5
    pixel_y = (lane >> 5).astype(F32) + 0.5
    rows_chunk = LANES // TILE_SIDE
    ones = jnp.ones((8, LANES), F32)

    def spread(cols, j):
        return jnp.broadcast_to(cols[:, j : j + 1], (8, LANES))

    def forward(g, carry):
        trans, color = carry
        at = pl.ds(pl.multiple_of(g * 8, 8), 8)
        cols = columns[at, :]
        cx, cy, qa, qb, qc, op, red, green, blue = [spread(cols, j) for j in range(9)]
        ex = pixel_x - cx
        ey0 = pixel_y - cy
        qaxx = qa * ex * ex
        qbx = qb * ex
        new_trans, new_color = [], []
        for c in range(chunks):
            ey = ey0 + float(c * rows_chunk)
            alpha = op * jnp.exp(qaxx + (qbx + qc * ey) * ey)
            keep = 1.0 - alpha
            run = jnp.where(sub >= 1, pltpu.roll(keep, 1, 0), 1.0)
            for s in (1, 2, 4):
                run = run * jnp.where(sub >= s, pltpu.roll(run, s, 0), 1.0)
            t = run * trans[c]
            after = t * keep
            new_trans.append(jnp.broadcast_to(after[7:8, :], (8, LANES)))
            part = slice(c * LANES, (c + 1) * LANES)
            alphas[at, part] = alpha
            transes[at, part] = t
            weight = alpha * t
            new_color.append(color[3 * c] + weight * red)
            new_color.append(color[3 * c + 1] + weight * green)
            new_color.append(color[3 * c + 2] + weight * blue)
        return new_trans, new_color

    zeros = jnp.zeros((8, LANES), F32)
    trans, color = lax.fori_loop(0, groups, forward, ([ones] * chunks, [zeros] * (3 * chunks)))

    totals = []
    for c in range(chunks):
        part = slice(c * LANES, (c + 1) * LANES)
        total = 0.0
        for k in range(3):
            shade = jnp.sum(color[3 * c + k], axis=0, keepdims=True) + trans[c][0:1, :] * back_ref[k]
            image_ref[k : k + 1, part] = shade
            miss = shade - target_ref[tile, k : k + 1, part]
            misses[k, :, part] = jnp.broadcast_to(miss, (8, LANES))
            total = total + miss * shade
        totals.append(jnp.broadcast_to(total, (8, LANES)))

    def backward(g, behind):
        at = pl.ds(pl.multiple_of(g * 8, 8), 8)
        cols = columns[at, :]
        cx, cy, red, green, blue = [spread(cols, j) for j in (0, 1, 6, 7, 8)]
        ex = pixel_x - cx
        ey0 = pixel_y - cy
        new_behind = []
        acc = [zeros] * 6
        for c in range(chunks):
            part = slice(c * LANES, (c + 1) * LANES)
            alpha = alphas[at, part]
            t = transes[at, part]
            m0, m1, m2 = misses[0, :, part], misses[1, :, part], misses[2, :, part]
            weight = alpha * t
            pull = m0 * red + m1 * green + m2 * blue
            run = weight * pull
            for s in (1, 2, 4):
                run = run + jnp.where(sub >= s, pltpu.roll(run, s, 0), 0.0)
            rest = behind[c] - run
            new_behind.append(jnp.broadcast_to(rest[7:8, :], (8, LANES)))
            grad = alpha * (t * pull - rest / (1.0 - alpha))
            ey = ey0 + float(c * rows_chunk)
            gy = grad * ey
            acc[0] = acc[0] + grad
            acc[1] = acc[1] + gy
            acc[2] = acc[2] + gy * ey
            acc[3] = acc[3] + weight * m0
            acc[4] = acc[4] + weight * m1
            acc[5] = acc[5] + weight * m2
        gx = acc[0] * ex
        fields = [acc[0], gx, acc[1], gx * ex, acc[1] * ex, acc[2], acc[3], acc[4], acc[5]]
        packed = zeros
        for j, field in enumerate(fields):
            packed = jnp.where(lane == j, jnp.sum(field, axis=1, keepdims=True), packed)
        sums[at, :] = packed
        return new_behind

    lax.fori_loop(0, groups, backward, totals)

    flat = sums[...].T
    s0, sx, sy, sxx, sxy, syy, d_red, d_green, d_blue = [flat[j : j + 1, :] for j in range(9)]
    d_x = conic_a * sx + conic_b * sy
    d_y = conic_b * sx + conic_c * sy
    d_a, d_b, d_c = -0.5 * sxx, -sxy, -0.5 * syy
    d_xx = -(conic_a * conic_a * d_a + conic_a * conic_b * d_b + conic_b * conic_b * d_c)
    d_yy = -(conic_b * conic_b * d_a + conic_b * conic_c * d_b + conic_c * conic_c * d_c)
    d_xy = -(
        2.0 * conic_a * conic_b * d_a
        + (conic_a * conic_c + conic_b * conic_b) * d_b
        + 2.0 * conic_b * conic_c * d_c
    )
    out = [first[j] * d_x + second[j] * d_y for j in range(3)]
    for j in range(3):
        d_var = first[j] * first[j] * d_xx + first[j] * second[j] * d_xy + second[j] * second[j] * d_yy
        out.append(2.0 * variance[j] * d_var)
    out += [s0 * (1.0 - opacity), d_red, d_green, d_blue, owner.astype(F32), row.astype(F32)]
    out.append(jnp.zeros((16 - len(out), entries), F32))
    grad_ref[...] = jnp.concatenate(out, axis=0)


def scatter_kernel(where_ref, grads_ref, out_ref):
    sources, _, entries = grads_ref.shape
    lines = out_ref.shape[0]
    highs = lines // 10
    me = where_ref[0]
    high_iota = lax.broadcasted_iota(jnp.int32, (highs, entries), 0)
    low_iota = lax.broadcasted_iota(jnp.int32, (LANES, entries), 0)
    out_ref[...] = jnp.zeros_like(out_ref)

    def add(s, carry):
        block = grads_ref[s]
        owner = block[10:11, :].astype(jnp.int32)
        row = block[11:12, :].astype(jnp.int32)
        onehot = jnp.where(low_iota == (row & (LANES - 1)), 1.0, 0.0).astype(BF16)
        mask = high_iota == jnp.where(owner == me, row >> 7, -1)
        placed = jnp.concatenate(
            [jnp.where(mask, block[p : p + 1, :], 0.0) for p in range(10)], axis=0
        )
        high = placed.astype(BF16)
        middle = (placed - high.astype(F32)).astype(BF16)
        dims = (((1,), (1,)), ((), ()))
        out_ref[...] += lax.dot_general(
            high, onehot, dims, preferred_element_type=F32
        ) + lax.dot_general(middle, onehot, dims, preferred_element_type=F32)
        return carry

    lax.fori_loop(0, sources, add, 0, unroll=min(sources, 4))


def adam_update(param, first, second, gradient):
    new_first = 0.9 * first + 0.1 * gradient
    new_second = 0.999 * second + 0.001 * gradient * gradient
    corrected = new_first / (1.0 - 0.9**10) / (jnp.sqrt(new_second / (1.0 - 0.999**10)) + 1e-08)
    return (param - 0.05 * corrected, new_first, new_second)


def body(
    positions, log_scales, opacity_logits, colors, first_moment, second_moment,
    cameras, background, target, tile_view, tile_length, list_owner, list_row,
):
    tiles_here, _, pixels = target.shape
    slab = list_row.shape[2]
    depth_count = lax.axis_size("depth")
    entries = slab * depth_count
    here = lax.axis_index("depth").astype(jnp.int32).reshape(1)
    home = lax.axis_index("tile").astype(jnp.int32).reshape(1)
    assert tiles_here == depth_count
    params = jnp.concatenate([positions, log_scales, opacity_logits, colors], axis=0)
    splats = params.shape[1]
    lines = 10 * splats // LANES
    named = jnp.stack([list_owner[0, :, :, 0], list_row[0]], axis=1)
    every, lists = exchange(
        [(params.reshape(lines, LANES), "tile", "gather"), (named, "depth", "spread")], "share", 1
    )
    smem = pl.BlockSpec(memory_space=pltpu.SMEM)
    vmem = pl.BlockSpec(memory_space=pltpu.VMEM)
    own_image, own_grad = pl.pallas_call(
        render_kernel,
        out_shape=[
            jax.ShapeDtypeStruct((3, pixels), F32),
            jax.ShapeDtypeStruct((16, entries), F32),
        ],
        in_specs=[smem] * 5 + [vmem] * 3,
        out_specs=[vmem] * 2,
        scratch_shapes=[
            pltpu.VMEM((lines, entries), F32),
            pltpu.VMEM((entries, pixels), F32),
            pltpu.VMEM((entries, pixels), F32),
            pltpu.VMEM((3, 8, pixels), F32),
            pltpu.VMEM((entries, LANES), F32),
            pltpu.VMEM((entries, LANES), F32),
        ],
        name="render",
        compiler_params=pltpu.CompilerParams(vmem_limit_bytes=60 << 20),
    )(here, tile_view, tile_length, cameras.reshape(-1), background, lists, every, target)
    grads, image = exchange(
        [(own_grad, "tile", "gather"), (own_image, "depth", "gather")], "collect", 2
    )
    partial = pl.pallas_call(
        scatter_kernel,
        out_shape=jax.ShapeDtypeStruct((lines, LANES), F32),
        in_specs=[smem, vmem],
        out_specs=vmem,
        name="scatter",
        compiler_params=pltpu.CompilerParams(vmem_limit_bytes=60 << 20),
    )(home, grads)
    (parts,) = exchange([(partial, "depth", "gather")], "reduce", 3)
    gradient = jnp.sum(parts, axis=0).reshape(10, splats)
    new_params, new_first, new_second = adam_update(params, first_moment, second_moment, gradient)
    return (image, new_params, new_first, new_second)


def solution(mesh):
    placed = (
        P(None, "tile"),
        P(None, "tile"),
        P(None, "tile"),
        P(None, "tile"),
        P(None, "tile"),
        P(None, "tile"),
        P(),
        P(),
        P("tile", None, None),
        P("tile"),
        P("tile"),
        P("depth", "tile", None, None),
        P("depth", "tile", None),
    )
    return jax.shard_map(
        body,
        mesh=mesh,
        in_specs=placed,
        out_specs=(P("tile", None, None), P(None, "tile"), P(None, "tile"), P(None, "tile")),
        check_vma=False,
    )
```

time: 200 us -> 77.3 us (0.39)
  Pallas kernels: 0 us -> 68.5 us
  local copies, waits for them, and re-layouts: 62.6 us -> 4.03 us
  waiting for transfers between devices: 36.4 us -> 0 us
  other arithmetic: 30.1 us -> 3.33 us
  matrix products: 20.8 us -> 0 us
  blocking collectives: 20.7 us -> 0 us
  starting transfers between devices: 14.1 us -> 0 us
  between operations: 14.6 us -> 0.77 us
    pallas_call x0 -> x5, Pallas kernels: none -> 68.5 us  [the longest x3 43 us: exchange(): pl.pallas_call(kernel, out_shape=outs, in_specs=[space] * count, out_spec...]
    slice x5 -> x0, local copies, waits for them, and re-layouts: 38.1 us -> none  [the longest x1 36.3 us: project(): cams[:, 1, 3]]
    psum x1 -> x0, waiting for transfers between devices: 22.6 us -> none  [body(): gradient = lax.psum(gradient, 'depth')]
    dot_general x6 -> x0, matrix products: 20.8 us -> none  [the longest x4 17.9 us: running_sum(): jnp.einsum('pbk,kj->pbj', blocks, triangle, precision=lax.Precision.HIGHEST)]
    all_to_all x2 -> x0, blocking collectives: 15.4 us -> none  [the longest x1 9.17 us: body(): lax.all_to_all(outgoing, 'tile', split_axis=1, concat_axis=1, tiled=True)]
    all_to_all x3 -> x0, starting transfers between devices: 14.1 us -> none  [the longest x1 7.31 us: body(): lax.all_to_all(request, 'tile', split_axis=1, concat_axis=1, tiled=True)]
    all_to_all x3 -> x0, waiting for transfers between devices: 13.8 us -> none  [the longest x1 5.89 us: body(): lax.all_to_all(screen, 'tile', split_axis=1, concat_axis=1, tiled=True)]
    scatter-add x1 -> x0, other arithmetic: 10.3 us -> none  [body(): gradient = jnp.zeros_like(params).at[:, rows_in].add(slot_grad)]
  transfers between devices with their start and end apart: 4 -> 0, of which waited for: 4 -> 0; matrix products, arithmetic and copies ran while one was open for 2% -> 0% of each run, Pallas kernels for 0% -> 0%
where the time goes in v1:
time: 77.3 us; the launch traced here: 76.7 us
  Pallas kernels  68.5 us (89%)
  local copies, waits for them, and re-layouts  4.03 us (5%)
  other arithmetic  3.33 us (4%)
    pallas_call x3, Pallas kernels, exchange(): pl.pallas_call(kernel, out_shape=outs, in_specs=[space] * count, out_spec...  43 us
    pallas_call x1, Pallas kernels, body(): pl.pallas_call(render_kernel, out_shape=[jax.ShapeDtypeStruct((3, pixels)...  22.7 us
    pallas_call x1, Pallas kernels, body(): pl.pallas_call(scatter_kernel, out_shape=jax.ShapeDtypeStruct((lines, LAN...  2.86 us
    unnamed x24, local copies, waits for them, and re-layouts  2.77 us

profile of v1, /device:TPU:0, one launch (start us, length us, event | category | flops | bytes accessed | tf_op | source)
XLA Modules:
  0.0 76.7 jit_solution(2974727052594020411)
XLA Ops:
  0.6 0.9 %pad_maximum_fusion = f32[10,2048]{1,0:T(8,128)S(1)} fusion(f32[3,2048]{1,0:T(4,128)} %param.16, f32[1,2048]{1,0:T(1,128)} %param.15, f32[3,2048]{1,0:T(4,128)} %param.14, f32[3,2048]{1,0:T(4,128)} %param.13), kind=kLoop, calls=%fused_computation.2 | loop fusion | flops 61440 | bytes 163840 | tf_op jit(solution)/shard_map/concatenate | solution.py:320
  1.5 0.7 reshape.25.refs_0_
  2.2 0.0 copy-done.10
  2.2 0.7 copy-done.9
  2.8 0.6 pad_add_fusion.refs_1_
  3.4 23.5 %share.1 = (f32[8,160,128]{2,1,0:T(8,128)}, s32[4,2,128]{2,1,0:T(2,128)}) custom-call(f32[160,128]{1,0:T(8,128)} %reshape.25.refs_0_, s32[4,2,128]{2,1,0:T(2,128)} %pad_add_fusion.refs_1_), custom_call_target="tpu_custom_call" | custom-call | tf_op jit(solution)/shard_map/share/pallas_call | solution.py:73
  27.0 0.7 copy.17.target_ref
  27.7 0.0 copy-done.8
  27.7 0.6 reshape.24.cam_ref
  28.3 22.7 %render.1 = (f32[3,1024]{1,0:T(4,128)}, f32[16,512]{1,0:T(8,128)}) custom-call(s32[1]{0:T(128)} %bitcast.where_ref, s32[4]{0:T(128)} %view_ref.1, s32[4]{0:T(128)} %length_ref.1, f32[32]{0:T(128)} %reshape.24.cam_ref, f32[3]{0:T(128)} %back_ref.1, s32[4,2,128]{2,1,0:T(2,128)} %get-tuple-element.10.list_ref, f32[8,160,128]{2,1,0:T(8,128)} %get-tuple-element.11.param_ref, ...), custom_call_target="tpu_custom_call" | custom-call | tf_op jit(solution)/shard_map/render/pallas_call | solution.py:329
  50.9 11.3 %collect.1 = (f32[8,16,512]{2,1,0:T(8,128)}, f32[4,3,1024]{2,1,0:T(4,128)}) custom-call(f32[16,512]{1,0:T(8,128)} %get-tuple-element.12.refs_0_, f32[3,1024]{1,0:T(4,128)} %get-tuple-element.13.refs_1_), custom_call_target="tpu_custom_call" | custom-call | tf_op jit(solution)/shard_map/collect/pallas_call | solution.py:73
  62.2 2.9 %scatter.1.refs_0_ = f32[160,128]{1,0:T(8,128)} custom-call(s32[1]{0:T(128)} %bitcast.3.where_ref, f32[8,16,512]{2,1,0:T(8,128)} %get-tuple-element.15.grads_ref), custom_call_target="tpu_custom_call" | custom-call | tf_op jit(solution)/shard_map/scatter/pallas_call | solution.py:351
  65.1 8.2 %reduce.1 = f32[4,160,128]{2,1,0:T(8,128)} custom-call(f32[160,128]{1,0:T(8,128)} %scatter.1.refs_0_), custom_call_target="tpu_custom_call" | custom-call | tf_op jit(solution)/shard_map/reduce/pallas_call | solution.py:73
  73.3 0.0 copy-start.4
  73.3 1.0 %reduce_sum.9 = f32[160,128]{1,0:T(8,128)S(1)} reduce(f32[4,160,128]{2,1,0:T(8,128)} %reduce.1, f32[]{:T(128)} %constant.9.clone.1), dimensions={0}, to_apply=%region_0.0 | reduce | flops 61440 | bytes 409604 | tf_op jit(solution)/shard_map/reduce_sum | solution.py:360
  74.4 0.0 copy-start
  74.4 0.0 copy-start.2
  74.4 0.0 copy-start.7
  74.5 0.7 copy-done
  75.1 0.0 copy-done.1
  75.1 0.0 copy-done.2
  75.2 0.8 %multiply_subtract_fusion = (f32[10,2048]{1,0:T(8,128)}, f32[10,2048]{1,0:T(8,128)}, f32[10,2048]{1,0:T(8,128)}) fusion(f32[3,2048]{1,0:T(4,128)S(1)} %copy-done, f32[1,2048]{1,0:T(1,128)S(1)} %copy-done.7, f32[3,2048]{1,0:T(4,128)S(1)} %copy-done.1, f32[3,2048]{1,0:T(4,128)S(1)} %copy-done.2, f32[10,2048]{1,0:T(8,128)S(1)} %reshape.27, ...), kind=kLoop, calls=%fused_computation.3 | loop fusion | flops 327680 | bytes 573440 | tf_op jit(solution)/shard_map/sub | solution.py:306
  76.0 0.0 copy-done.5
  76.0 0.7 copy.18
  (12 shorter events, 0.0 us)
Async XLA Ops:
  1.5 0.7 copy-start.10
  2.2 0.7 copy-start.9
  3.4 23.5 %copy-start.6 = (f32[4,3,1024]{2,0,1:T(4,128)S(1)}, f32[4,3,1024]{2,0,1:T(4,128)}, u32[]{:S(2)}) copy-start(f32[4,3,1024]{2,0,1:T(4,128)} %param.21) | copy-start | bytes 147460
  27.0 0.7 copy-start.8
  73.3 1.1 %copy-start.3 = (f32[10,2048]{1,0:T(8,128)S(1)}, f32[10,2048]{1,0:T(8,128)}, u32[]{:S(2)}) copy-start(f32[10,2048]{1,0:T(8,128)} %param.17) | copy-start | bytes 245764
  73.3 1.1 %copy-start.4 = (f32[10,2048]{1,0:T(8,128)S(1)}, f32[10,2048]{1,0:T(8,128)}, u32[]{:S(2)}) copy-start(f32[10,2048]{1,0:T(8,128)} %param.18) | copy-start | bytes 245764
  74.4 0.8 copy-start
  74.4 0.8 %copy-start.1 = (f32[3,2048]{1,0:T(4,128)S(1)}, f32[3,2048]{1,0:T(4,128)}, u32[]{:S(2)}) copy-start(f32[3,2048]{1,0:T(4,128)} %param.14) | copy-start | bytes 73732
  74.4 0.8 %copy-start.2 = (f32[3,2048]{1,0:T(4,128)S(1)}, f32[3,2048]{1,0:T(4,128)}, u32[]{:S(2)}) copy-start(f32[3,2048]{1,0:T(4,128)} %param.13) | copy-start | bytes 73732
  74.4 0.8 copy-start.7
  75.2 0.8 %copy-start.5 = (f32[4,3,1024]{2,1,0:T(4,128)S(1)}, f32[4,3,1024]{2,1,0:T(4,128)}, u32[]{:S(2)}) copy-start(f32[4,3,1024]{2,1,0:T(4,128)} %get-tuple-element.16) | copy-start | bytes 147460

commit v2 on v1

v2 whole, which is shorter than its diff:
```python
import functools

import jax
import jax.numpy as jnp
from jax import lax
from jax.experimental import pallas as pl
from jax.experimental.pallas import tpu as pltpu
from jax.sharding import PartitionSpec as P

TILE_SIDE = 32
LANES = 128
MESH = pl.DeviceIdType.MESH
F32 = jnp.float32
BF16 = jnp.bfloat16


def greet(peers):
    barrier = pltpu.get_barrier_semaphore()
    for peer in peers:
        pl.semaphore_signal(barrier, inc=1, device_id=peer, device_id_type=MESH)
    pl.semaphore_wait(barrier, len(peers))


def remote(source, target, send, receive, peer):
    return pltpu.make_async_remote_copy(
        src_ref=source, dst_ref=target, send_sem=send, recv_sem=receive,
        device_id=peer, device_id_type=MESH,
    )


def entry_rows(lists_ref, slot):
    slabs = lists_ref.shape[1]
    owner = jnp.concatenate([lists_ref[slot, d, 0:1, :] for d in range(slabs)], axis=1)
    row = jnp.concatenate([lists_ref[slot, d, 1:2, :] for d in range(slabs)], axis=1)
    return owner, row


def split3(x):
    high = x.astype(BF16)
    rest = x - high.astype(F32)
    middle = rest.astype(BF16)
    low = (rest - middle.astype(F32)).astype(BF16)
    return high, middle, low


def fetch_kernel(
    tiles, depths, named_ref, param_ref, lists_ref, entry_ref,
    high_ref, low_ref, answers, got, ask_send, ask_recv, own_sem, send, receive,
):
    lines = param_ref.shape[0]
    highs = lines // 10
    slabs, _, slab = named_ref.shape
    entries = slabs * slab
    me_t, me_d = lax.axis_index("tile"), lax.axis_index("depth")
    steps = [(a, b) for a in range(tiles - 1, -1, -1) for b in range(depths) if a or b]

    def to(a, b):
        return {"tile": lax.rem(me_t + a, tiles), "depth": lax.rem(me_d + b, depths)}

    greet([to(a, b) for a, b in steps])
    for a, b in steps:
        remote(
            named_ref.at[lax.rem(me_d + b, depths)], lists_ref.at[me_t, me_d],
            ask_send.at[a, b], ask_recv.at[a, b], to(a, b),
        ).start()
    own = pltpu.make_async_copy(named_ref.at[me_d], lists_ref.at[me_t, me_d], own_sem)
    own.start()
    high, middle, low = split3(param_ref[...])
    high_ref[...] = jnp.concatenate([high, middle], axis=1)
    low_ref[...] = low
    low_iota = lax.broadcasted_iota(jnp.int32, (LANES, entries), 0)
    high_iota = lax.broadcasted_iota(jnp.int32, (highs, entries), 0)

    def asked(a, b):
        return remote(
            named_ref.at[me_d], lists_ref.at[me_t, me_d],
            ask_send.at[a, b], ask_recv.at[a, b], to(a, b),
        )

    def answer(slot):
        owner, row = entry_rows(lists_ref, slot)
        onehot = jnp.where(low_iota == (row & (LANES - 1)), 1.0, 0.0).astype(BF16)
        twice = jnp.concatenate([onehot, onehot], axis=0)
        found = jnp.dot(high_ref[...], twice, preferred_element_type=F32) + jnp.dot(
            low_ref[...], onehot, preferred_element_type=F32
        )
        mask = high_iota == jnp.where(owner == me_t, row >> 7, -1)
        return jnp.concatenate(
            [
                jnp.sum(
                    jnp.where(mask, found[p * highs : (p + 1) * highs], 0.0), axis=0, keepdims=True
                )
                for p in range(10)
            ],
            axis=0,
        )

    def put(ref, step, rows):
        for j in range(slabs):
            ref[step, j * 10 : (j + 1) * 10, :] = rows[:, j * slab : (j + 1) * slab]

    def back(step):
        peer = {"tile": lax.rem(me_t - step + tiles, tiles)}
        return remote(answers.at[step], got.at[step], send.at[step], receive.at[step], peer)

    def serve(step, carry):
        for b in range(depths):
            asked(step, b).wait_recv()
        put(answers, step, answer(lax.rem(me_t - step + tiles, tiles)))
        back(step).start()
        return carry

    lax.fori_loop(1, tiles, serve, 0, unroll=tiles - 1 if tiles <= 8 else 1)
    own.wait()
    for b in range(1, depths):
        asked(0, b).wait_recv()
    put(got, 0, answer(me_t))
    for a, b in steps:
        asked(a, b).wait_send()
    entry_ref[...] = got[0]

    def take(step, carry):
        back(step).wait()
        entry_ref[...] += got[step]
        return carry

    lax.fori_loop(1, tiles, take, 0)


def render_kernel(
    where_ref, view_ref, length_ref, cam_ref, back_ref,
    entry_ref, target_ref,
    image_ref, grad_ref,
    alphas, transes, misses, carries, columns, sums,
):
    slabs = target_ref.shape[0]
    slab = entry_ref.shape[1]
    entries = slabs * slab
    pixels = target_ref.shape[2]
    chunks = pixels // LANES
    groups = entries // 8
    tile = where_ref[0]
    length = length_ref[tile]
    view = view_ref[tile]
    values = [
        jnp.concatenate([entry_ref[j * 10 + p : j * 10 + p + 1, :] for j in range(slabs)], axis=1)
        for p in range(10)
    ]

    base = view * 8
    first = [cam_ref[base + j] for j in range(4)]
    second = [cam_ref[base + 4 + j] for j in range(4)]
    variance = [jnp.exp(2.0 * values[3 + j]) for j in range(3)]
    half = 0.5 * TILE_SIDE
    center_x = first[0] * values[0] + first[1] * values[1] + first[2] * values[2] + first[3] + half
    center_y = second[0] * values[0] + second[1] * values[1] + second[2] * values[2] + second[3] + half
    cov_xx = sum(first[j] * first[j] * variance[j] for j in range(3)) + 0.3
    cov_xy = sum(first[j] * second[j] * variance[j] for j in range(3))
    cov_yy = sum(second[j] * second[j] * variance[j] for j in range(3)) + 0.3
    determinant = cov_xx * cov_yy - cov_xy * cov_xy
    conic_a = cov_yy / determinant
    conic_b = -cov_xy / determinant
    conic_c = cov_xx / determinant
    opacity = 1.0 / (1.0 + jnp.exp(-values[6]))
    place = lax.broadcasted_iota(jnp.int32, (1, entries), 1)
    shown = jnp.where(place < length, opacity, 0.0)
    rows = [center_x, center_y, -0.5 * conic_a, -conic_b, -0.5 * conic_c, shown] + values[7:10]
    table = jnp.concatenate(rows + [jnp.zeros((LANES - len(rows), entries), F32)], axis=0)
    columns[...] = table.T

    lane = lax.broadcasted_iota(jnp.int32, (8, LANES), 1)
    sub = lax.broadcasted_iota(jnp.int32, (8, LANES), 0)
    pixel_x = (lane & (TILE_SIDE - 1)).astype(F32) + 0.5
    pixel_y = (lane >> 5).astype(F32) + 0.5
    rows_chunk = LANES // TILE_SIDE
    ones = jnp.ones((8, LANES), F32)

    def spread(cols, j):
        return jnp.broadcast_to(cols[:, j : j + 1], (8, LANES))

    def forward(g, carry):
        trans, color = carry
        at = pl.ds(pl.multiple_of(g * 8, 8), 8)
        cols = columns[pl.ds(g, 8, stride=groups), :]
        cx, cy, qa, qb, qc, op, red, green, blue = [spread(cols, j) for j in range(9)]
        ex = pixel_x - cx
        ey0 = pixel_y - cy
        qaxx = qa * ex * ex
        qbx = qb * ex
        new_trans, new_color = [], []
        for c in range(chunks):
            ey = ey0 + float(c * rows_chunk)
            alpha = op * jnp.exp(qaxx + (qbx + qc * ey) * ey)
            t = trans[c]
            part = slice(c * LANES, (c + 1) * LANES)
            alphas[at, part] = alpha
            transes[at, part] = t
            weight = alpha * t
            new_trans.append(t - weight)
            new_color.append(color[3 * c] + weight * red)
            new_color.append(color[3 * c + 1] + weight * green)
            new_color.append(color[3 * c + 2] + weight * blue)
        return new_trans, new_color

    zeros = jnp.zeros((8, LANES), F32)
    trans, color = lax.fori_loop(
        0, groups, forward, ([ones] * chunks, [zeros] * (3 * chunks)), unroll=2
    )

    behinds = []
    for c in range(chunks):
        part = slice(c * LANES, (c + 1) * LANES)
        run = jnp.where(sub >= 1, pltpu.roll(trans[c], 1, 0), 1.0)
        for s in (1, 2, 4):
            run = run * jnp.where(sub >= s, pltpu.roll(run, s, 0), 1.0)
        carries[:, part] = run
        left = (run * trans[c])[7:8, :]
        total = 0.0
        pulled = zeros
        for k in range(3):
            lit = run * color[3 * c + k]
            shade = jnp.sum(lit, axis=0, keepdims=True) + left * back_ref[k]
            image_ref[k : k + 1, part] = shade
            miss = shade - target_ref[tile, k : k + 1, part]
            misses[k, :, part] = jnp.broadcast_to(miss, (8, LANES))
            total = total + miss * shade
            pulled = pulled + miss * lit
        ahead = jnp.where(sub >= 1, pltpu.roll(pulled, 1, 0), 0.0)
        for s in (1, 2, 4):
            ahead = ahead + jnp.where(sub >= s, pltpu.roll(ahead, s, 0), 0.0)
        behinds.append(total - ahead)

    def backward(g, behind):
        at = pl.ds(pl.multiple_of(g * 8, 8), 8)
        spaced = pl.ds(g, 8, stride=groups)
        cols = columns[spaced, :]
        cx, cy, red, green, blue = [spread(cols, j) for j in (0, 1, 6, 7, 8)]
        ex = pixel_x - cx
        ey0 = pixel_y - cy
        new_behind = []
        acc = [zeros] * 6
        for c in range(chunks):
            part = slice(c * LANES, (c + 1) * LANES)
            alpha = alphas[at, part]
            t = transes[at, part] * carries[:, part]
            m0, m1, m2 = misses[0, :, part], misses[1, :, part], misses[2, :, part]
            weight = alpha * t
            pull = m0 * red + m1 * green + m2 * blue
            rest = behind[c] - weight * pull
            new_behind.append(rest)
            grad = weight * pull - rest * (alpha / (1.0 - alpha))
            ey = ey0 + float(c * rows_chunk)
            gy = grad * ey
            acc[0] = acc[0] + grad
            acc[1] = acc[1] + gy
            acc[2] = acc[2] + gy * ey
            acc[3] = acc[3] + weight * m0
            acc[4] = acc[4] + weight * m1
            acc[5] = acc[5] + weight * m2
        gx = acc[0] * ex
        fields = [acc[0], gx, acc[1], gx * ex, acc[1] * ex, acc[2], acc[3], acc[4], acc[5]]
        packed = zeros
        for j, field in enumerate(fields):
            packed = jnp.where(lane == j, jnp.sum(field, axis=1, keepdims=True), packed)
        sums[spaced, :] = packed
        return new_behind

    lax.fori_loop(0, groups, backward, behinds, unroll=2)

    flat = sums[...].T
    s0, sx, sy, sxx, sxy, syy, d_red, d_green, d_blue = [flat[j : j + 1, :] for j in range(9)]
    d_x = conic_a * sx + conic_b * sy
    d_y = conic_b * sx + conic_c * sy
    d_a, d_b, d_c = -0.5 * sxx, -sxy, -0.5 * syy
    d_xx = -(conic_a * conic_a * d_a + conic_a * conic_b * d_b + conic_b * conic_b * d_c)
    d_yy = -(conic_b * conic_b * d_a + conic_b * conic_c * d_b + conic_c * conic_c * d_c)
    d_xy = -(
        2.0 * conic_a * conic_b * d_a
        + (conic_a * conic_c + conic_b * conic_b) * d_b
        + 2.0 * conic_b * conic_c * d_c
    )
    out = [first[j] * d_x + second[j] * d_y for j in range(3)]
    for j in range(3):
        d_var = first[j] * first[j] * d_xx + first[j] * second[j] * d_xy + second[j] * second[j] * d_yy
        out.append(2.0 * variance[j] * d_var)
    out += [s0 * (1.0 - opacity), d_red, d_green, d_blue]
    out = jnp.concatenate(out, axis=0)
    for j in range(slabs):
        grad_ref[j * 10 : (j + 1) * 10, :] = out[:, j * slab : (j + 1) * slab]


def collect_kernel(
    tiles, depths, own_ref, image_ref, lists_ref, out_ref, images_ref,
    inbox, partial, pieces, mine,
    send, receive, image_send, image_recv, image_own, cut_send, cut_recv, all_send, all_recv,
):
    lines = out_ref.shape[0]
    highs = lines // 10
    quarter = lines // depths
    slabs, slab = lists_ref.shape[1], lists_ref.shape[3]
    entries = slabs * slab
    me_t, me_d = lax.axis_index("tile"), lax.axis_index("depth")

    def along(step):
        return {"depth": lax.rem(me_d + step, depths)}

    def across(step):
        return {"tile": lax.rem(me_t + step, tiles)}

    def grads(step):
        return remote(own_ref, inbox.at[step], send.at[step], receive.at[step], across(step))

    greet([across(s) for s in range(1, tiles)] + [along(s) for s in range(1, depths)])
    for step in range(tiles - 1, 0, -1):
        grads(step).start()
    image_copies = [
        remote(image_ref, images_ref.at[me_d], image_send.at[s], image_recv.at[s], along(s))
        for s in range(1, depths)
    ]
    image_copies.append(pltpu.make_async_copy(image_ref, images_ref.at[me_d], image_own))
    for copy in image_copies:
        copy.start()

    high_iota = lax.broadcasted_iota(jnp.int32, (highs, entries), 0)
    low_iota = lax.broadcasted_iota(jnp.int32, (LANES, entries), 0)

    def placed(block, slot):
        owner, row = entry_rows(lists_ref, slot)
        onehot = jnp.where(low_iota == (row & (LANES - 1)), 1.0, 0.0).astype(BF16)
        mask = high_iota == jnp.where(owner == me_t, row >> 7, -1)
        wide = jnp.concatenate([block[j * 10 : (j + 1) * 10, :] for j in range(slabs)], axis=1)
        spots = jnp.concatenate(
            [jnp.where(mask, wide[p : p + 1, :], 0.0) for p in range(10)], axis=0
        )
        high = spots.astype(BF16)
        middle = (spots - high.astype(F32)).astype(BF16)
        dims = (((1,), (1,)), ((), ()))
        return lax.dot_general(
            high, onehot, dims, preferred_element_type=F32
        ) + lax.dot_general(middle, onehot, dims, preferred_element_type=F32)

    partial[...] = placed(own_ref[...], me_t)

    def add(step, carry):
        grads(step).wait()
        partial[...] += placed(inbox[step], lax.rem(me_t - step + tiles, tiles))
        return carry

    lax.fori_loop(1, tiles, add, 0, unroll=tiles - 1 if tiles <= 8 else 1)
    for copy in image_copies:
        copy.wait()

    def rows_of(index):
        return pl.ds(pl.multiple_of(index * quarter, 8), quarter)

    cuts = [
        remote(
            partial.at[rows_of(lax.rem(me_d + s, depths))], pieces.at[s],
            cut_send.at[s], cut_recv.at[s], along(s),
        )
        for s in range(1, depths)
    ]
    for copy in cuts:
        copy.start()
    total = partial[rows_of(me_d), :]
    for s, copy in enumerate(cuts):
        copy.wait()
        total = total + pieces[s + 1]
    mine[...] = total
    shares = [
        remote(mine, out_ref.at[rows_of(me_d)], all_send.at[s], all_recv.at[s], along(s))
        for s in range(1, depths)
    ]
    for copy in shares:
        copy.start()
    out_ref[rows_of(me_d), :] = total
    for copy in shares:
        copy.wait()


def adam_update(param, first, second, gradient):
    new_first = 0.9 * first + 0.1 * gradient
    new_second = 0.999 * second + 0.001 * gradient * gradient
    corrected = new_first / (1.0 - 0.9**10) / (jnp.sqrt(new_second / (1.0 - 0.999**10)) + 1e-08)
    return (param - 0.05 * corrected, new_first, new_second)


def body(
    positions, log_scales, opacity_logits, colors, first_moment, second_moment,
    cameras, background, target, tile_view, tile_length, list_owner, list_row,
):
    tiles_here, _, pixels = target.shape
    slab = list_row.shape[2]
    depth_count = lax.axis_size("depth")
    entries = slab * depth_count
    here = lax.axis_index("depth").astype(jnp.int32).reshape(1)
    assert tiles_here == depth_count
    params = jnp.concatenate([positions, log_scales, opacity_logits, colors], axis=0)
    splats = params.shape[1]
    lines = 10 * splats // LANES
    named = jnp.stack([list_owner[0, :, :, 0], list_row[0]], axis=1)
    tile_count = lax.axis_size("tile")
    assert 10 * slab * depth_count % LANES == 0 and slab == LANES
    smem = pl.BlockSpec(memory_space=pltpu.SMEM)
    vmem = pl.BlockSpec(memory_space=pltpu.VMEM)
    dma = pltpu.SemaphoreType.DMA
    block = (10 * depth_count, slab)
    limit = 60 << 20
    lists, entry = pl.pallas_call(
        functools.partial(fetch_kernel, tile_count, depth_count),
        out_shape=[
            jax.ShapeDtypeStruct((tile_count, depth_count, 2, slab), jnp.int32),
            jax.ShapeDtypeStruct(block, F32),
        ],
        in_specs=[vmem] * 2,
        out_specs=[vmem] * 2,
        scratch_shapes=[
            pltpu.VMEM((lines, 2 * LANES), BF16),
            pltpu.VMEM((lines, LANES), BF16),
            pltpu.VMEM((tile_count,) + block, F32),
            pltpu.VMEM((tile_count,) + block, F32),
            dma((tile_count, depth_count)),
            dma((tile_count, depth_count)),
            dma,
            dma((tile_count,)),
            dma((tile_count,)),
        ],
        name="fetch",
        compiler_params=pltpu.CompilerParams(
            collective_id=1, has_side_effects=True, vmem_limit_bytes=limit
        ),
    )(named, params.reshape(lines, LANES))
    own_image, own_grad = pl.pallas_call(
        render_kernel,
        out_shape=[
            jax.ShapeDtypeStruct((3, pixels), F32),
            jax.ShapeDtypeStruct(block, F32),
        ],
        in_specs=[smem] * 5 + [vmem] * 2,
        out_specs=[vmem] * 2,
        scratch_shapes=[
            pltpu.VMEM((entries, pixels), F32),
            pltpu.VMEM((entries, pixels), F32),
            pltpu.VMEM((3, 8, pixels), F32),
            pltpu.VMEM((8, pixels), F32),
            pltpu.VMEM((entries, LANES), F32),
            pltpu.VMEM((entries, LANES), F32),
        ],
        name="render",
        compiler_params=pltpu.CompilerParams(vmem_limit_bytes=limit),
    )(here, tile_view, tile_length, cameras.reshape(-1), background, entry, target)
    quarter = lines // depth_count
    total, image = pl.pallas_call(
        functools.partial(collect_kernel, tile_count, depth_count),
        out_shape=[
            jax.ShapeDtypeStruct((lines, LANES), F32),
            jax.ShapeDtypeStruct((depth_count, 3, pixels), F32),
        ],
        in_specs=[vmem] * 3,
        out_specs=[vmem] * 2,
        scratch_shapes=[
            pltpu.VMEM((tile_count,) + block, F32),
            pltpu.VMEM((lines, LANES), F32),
            pltpu.VMEM((depth_count, quarter, LANES), F32),
            pltpu.VMEM((quarter, LANES), F32),
            dma((tile_count,)),
            dma((tile_count,)),
            dma((depth_count,)),
            dma((depth_count,)),
            dma,
            dma((depth_count,)),
            dma((depth_count,)),
            dma((depth_count,)),
            dma((depth_count,)),
        ],
        name="collect",
        compiler_params=pltpu.CompilerParams(
            collective_id=2, has_side_effects=True, vmem_limit_bytes=limit
        ),
    )(own_grad, own_image, lists)
    gradient = total.reshape(10, splats)
    new_params, new_first, new_second = adam_update(params, first_moment, second_moment, gradient)
    return (image, new_params, new_first, new_second)


def solution(mesh):
    placed = (
        P(None, "tile"),
        P(None, "tile"),
        P(None, "tile"),
        P(None, "tile"),
        P(None, "tile"),
        P(None, "tile"),
        P(),
        P(),
        P("tile", None, None),
        P("tile"),
        P("tile"),
        P("depth", "tile", None, None),
        P("depth", "tile", None),
    )
    return jax.shard_map(
        body,
        mesh=mesh,
        in_specs=placed,
        out_specs=(P("tile", None, None), P(None, "tile"), P(None, "tile"), P(None, "tile")),
        check_vma=False,
    )
```

time: 77.3 us -> 55.8 us (0.72)
  Pallas kernels: 68.5 us -> 47.1 us
  local copies, waits for them, and re-layouts: 4.03 us -> 6.01 us
  other arithmetic: 3.33 us -> 1.48 us
    pallas_call x4 -> x2, Pallas kernels: 45.9 us -> 35 us  [the longest x1 18.2 us: body(): pl.pallas_call(functools.partial(fetch_kernel, tile_count, depth_count),...]
    pallas_call x1, Pallas kernels: 22.7 us -> 12.2 us  [body(): pl.pallas_call(render_kernel, out_shape=[jax.ShapeDtypeStruct((3, pixels)...]
    reduce_sum x1 -> x0, other arithmetic: 1.04 us -> none  [body(): gradient = jnp.sum(parts, axis=0).reshape(10, splats)]
    unnamed x24 -> x20, local copies, waits for them, and re-layouts: 2.77 us -> 3.78 us
    reshape x1, local copies, waits for them, and re-layouts: 0.02 us -> 0.94 us  [body(): gradient = total.reshape(10, splats)]
    concatenate x1, other arithmetic: 0.86 us -> 0.05 us  [body(): jnp.concatenate([positions, log_scales, opacity_logits, colors], axis=0)]
where the time goes in v2:
time: 55.8 us; the launch traced here: 55.3 us
  Pallas kernels  47.1 us (84%)
  local copies, waits for them, and re-layouts  6.01 us (11%)
  other arithmetic  1.48 us (3%)
  between operations  0.72 us (1%)
    pallas_call x1, Pallas kernels, body(): pl.pallas_call(functools.partial(fetch_kernel, tile_count, depth_count),...  18.2 us
    pallas_call x1, Pallas kernels, body(): pl.pallas_call(functools.partial(collect_kernel, tile_count, depth_count)...  16.7 us
    pallas_call x1, Pallas kernels, body(): pl.pallas_call(render_kernel, out_shape=[jax.ShapeDtypeStruct((3, pixels)...  12.2 us
    unnamed x20, local copies, waits for them, and re-layouts  3.78 us

profile of v2, /device:TPU:0, one launch (start us, length us, event | category | flops | bytes accessed | tf_op | source)
XLA Modules:
  0.0 55.3 jit_solution(13364479834223338714)
XLA Ops:
  0.6 0.0 copy-start.6
  0.6 0.7 %copy-done.6 = f32[4,2,4]{2,1,0:T(2,128)S(1)} copy-done((f32[4,2,4]{2,1,0:T(2,128)S(1)}, f32[4,2,4]{2,1,0:T(2,128)}, u32[]{:S(2)}) %copy-start.6) | copy-done | bytes 152
  1.3 0.0 copy-start.7
  1.3 0.0 copy-start.8
  1.3 0.6 %reshape.21.cam_ref = f32[32]{0:T(128)} reshape(f32[4,2,4]{2,1,0:T(2,128)S(1)} %copy-done.6) | data formatting | bytes 256 | tf_op jit(solution)/shard_map/reshape | solution.py:451
  2.0 0.0 copy-done.7
  2.0 0.0 copy-done.8
  2.0 0.6 %pad_add_fusion.named_ref = s32[4,2,128]{2,1,0:T(2,128)} fusion(s32[4,1,128]{2,1,0:T(1,128)S(1)} %bitcast.3, s32[4,1,128]{2,1,0:T(1,128)S(1)} %bitcast.4), kind=kLoop, calls=%fused_computation.5 | loop fusion | flops 1024 | bytes 8192 | tf_op jit(solution)/shard_map/stack | solution.py:401
  2.6 1.5 %copy.17.target_ref = f32[4,3,1024]{2,1,0:T(4,128)} copy(f32[4,3,1024]{2,0,1:T(4,128)} %param.21) | data formatting | bytes 98304 | tf_op args[8]
  4.1 0.0 copy-done
  4.1 0.0 copy-done.1
  4.1 0.0 copy-done.2
  4.1 0.0 copy-done.5
  4.1 0.1 pad_maximum_fusion
  4.2 0.7 %reshape.22.param_ref = f32[160,128]{1,0:T(8,128)} reshape(f32[10,2048]{1,0:T(8,128)S(1)} %pad_maximum_fusion) | data formatting | bytes 163840 | tf_op jit(solution)/shard_map/reshape | solution.py:432
  4.9 18.2 %fetch.1 = (s32[8,4,2,128]{3,2,1,0:T(2,128)}, f32[40,128]{1,0:T(8,128)}) custom-call(s32[4,2,128]{2,1,0:T(2,128)} %pad_add_fusion.named_ref, f32[160,128]{1,0:T(8,128)} %reshape.22.param_ref), custom_call_target="tpu_custom_call" | custom-call | tf_op jit(solution)/shard_map/fetch/pallas_call | solution.py:409
  23.1 12.2 %render.1 = (f32[3,1024]{1,0:T(4,128)}, f32[40,128]{1,0:T(8,128)}) custom-call(s32[1]{0:T(128)} %bitcast.where_ref, s32[4]{0:T(128)} %view_ref.1, s32[4]{0:T(128)} %length_ref.1, f32[32]{0:T(128)} %reshape.21.cam_ref, f32[3]{0:T(128)} %back_ref.1, f32[40,128]{1,0:T(8,128)} %get-tuple-element.10.entry_ref, f32[4,3,1024]{2,1,0:T(4,128)} %copy.17.target_ref), custom_call_target="tpu_custom_call" | custom-call | tf_op jit(solution)/shard_map/render/pallas_call | solution.py:433
  35.3 16.7 %collect.1 = (f32[160,128]{1,0:T(8,128)}, f32[4,3,1024]{2,1,0:T(4,128)}) custom-call(f32[40,128]{1,0:T(8,128)} %get-tuple-element.11.own_ref, f32[3,1024]{1,0:T(4,128)} %get-tuple-element.12.image_ref, s32[8,4,2,128]{3,2,1,0:T(2,128)} %get-tuple-element.13.lists_ref), custom_call_target="tpu_custom_call" | custom-call | tf_op jit(solution)/shard_map/collect/pallas_call | solution.py:453
  52.0 0.0 copy-start.4
  52.0 1.5 %copy.18 = f32[4,3,1024]{2,0,1:T(4,128)} copy(f32[4,3,1024]{2,1,0:T(4,128)} %get-tuple-element.16) | data formatting | bytes 98304
  53.6 0.9 %reshape.23 = f32[10,2048]{1,0:T(8,128)S(1)} reshape(f32[160,128]{1,0:T(8,128)} %get-tuple-element.15) | data formatting | bytes 163840 | tf_op jit(solution)/shard_map/reshape | solution.py:481
  54.5 0.0 copy-done.4
  54.5 0.0 copy-done.3
  54.5 0.8 %multiply_subtract_fusion = (f32[10,2048]{1,0:T(8,128)}, f32[10,2048]{1,0:T(8,128)}, f32[10,2048]{1,0:T(8,128)}) fusion(f32[3,2048]{1,0:T(4,128)S(1)} %copy-done, f32[1,2048]{1,0:T(1,128)S(1)} %copy-done.5, f32[3,2048]{1,0:T(4,128)S(1)} %copy-done.1, f32[3,2048]{1,0:T(4,128)S(1)} %copy-done.2, f32[10,2048]{1,0:T(8,128)S(1)} %reshape.23, ...), kind=kLoop, calls=%fused_computation.3 | loop fusion | flops 327680 | bytes 573440 | tf_op jit(solution)/shard_map/sub | solution.py:385
  (5 shorter events, 0.0 us)
Async XLA Ops:
  0.6 0.7 %copy-start.6 = (f32[4,2,4]{2,1,0:T(2,128)S(1)}, f32[4,2,4]{2,1,0:T(2,128)}, u32[]{:S(2)}) copy-start(f32[4,2,4]{2,1,0:T(2,128)} %param.19) | copy-start | bytes 388
  1.3 0.7 %copy-start.7 = (s32[1,4,128]{2,1,0:T(4,128)S(1)}, s32[1,4,128]{2,1,0:T(4,128)}, u32[]{:S(2)}) copy-start(s32[1,4,128]{2,1,0:T(4,128)} %param.25) | copy-start | bytes 6148
  1.3 0.7 %copy-start.8 = (s32[1,4,128,1]{2,3,1,0:T(1,128)S(1)}, s32[1,4,128,1]{2,3,1,0:T(1,128)}, u32[]{:S(2)}) copy-start(s32[1,4,128,1]{2,3,1,0:T(1,128)} %param.24) | copy-start | bytes 6148
  2.6 1.5 %copy-start = (f32[3,2048]{1,0:T(4,128)S(1)}, f32[3,2048]{1,0:T(4,128)}, u32[]{:S(2)}) copy-start(f32[3,2048]{1,0:T(4,128)} %param.16) | copy-start | bytes 73732
  2.6 1.5 %copy-start.1 = (f32[3,2048]{1,0:T(4,128)S(1)}, f32[3,2048]{1,0:T(4,128)}, u32[]{:S(2)}) copy-start(f32[3,2048]{1,0:T(4,128)} %param.14) | copy-start | bytes 73732
  2.6 1.5 %copy-start.2 = (f32[3,2048]{1,0:T(4,128)S(1)}, f32[3,2048]{1,0:T(4,128)}, u32[]{:S(2)}) copy-start(f32[3,2048]{1,0:T(4,128)} %param.13) | copy-start | bytes 73732
  2.6 1.5 %copy-start.5 = (f32[1,2048]{1,0:T(1,128)S(1)}, f32[1,2048]{1,0:T(1,128)}, u32[]{:S(2)}) copy-start(f32[1,2048]{1,0:T(1,128)} %param.15) | copy-start | bytes 24580
  52.0 2.5 %copy-start.4 = (f32[10,2048]{1,0:T(8,128)S(1)}, f32[10,2048]{1,0:T(8,128)}, u32[]{:S(2)}) copy-start(f32[10,2048]{1,0:T(8,128)} %param.18) | copy-start | bytes 245764
  53.6 1.0 %copy-start.3 = (f32[10,2048]{1,0:T(8,128)S(1)}, f32[10,2048]{1,0:T(8,128)}, u32[]{:S(2)}) copy-start(f32[10,2048]{1,0:T(8,128)} %param.17) | copy-start | bytes 245764

commit v3 on v2

--- a/solution.py
+++ b/solution.py
@@ -44,13 +44,24 @@
 
 
 def fetch_kernel(
-    tiles, depths, named_ref, param_ref, lists_ref, entry_ref,
-    high_ref, low_ref, answers, got, ask_send, ask_recv, own_sem, send, receive,
+    tiles, depths, owner_ref, row_ref, place_ref, scale_ref, logit_ref, color_ref,
+    lists_ref, entry_ref,
+    named_ref, param_ref, high_ref, low_ref, answers, got, ask_send, ask_recv, own_sem, send, receive,
 ):
     lines = param_ref.shape[0]
     highs = lines // 10
     slabs, _, slab = named_ref.shape
     entries = slabs * slab
+    for q in range(slabs):
+        named_ref[q, 0:1, :] = owner_ref[q]
+        named_ref[q, 1:2, :] = row_ref[q : q + 1, :]
+    param = 0
+    for ref in (place_ref, scale_ref, logit_ref, color_ref):
+        for k in range(ref.shape[0]):
+            for h in range(highs):
+                line = param * highs + h
+                param_ref[line : line + 1, :] = ref[k : k + 1, h * LANES : (h + 1) * LANES]
+            param += 1
     me_t, me_d = lax.axis_index("tile"), lax.axis_index("depth")
     steps = [(a, b) for a in range(tiles - 1, -1, -1) for b in range(depths) if a or b]
 
@@ -133,7 +144,7 @@
     image_ref, grad_ref,
     alphas, transes, misses, carries, columns, sums,
 ):
-    slabs = target_ref.shape[0]
+    slabs = target_ref.shape[1]
     slab = entry_ref.shape[1]
     entries = slabs * slab
     pixels = target_ref.shape[2]
@@ -147,9 +158,8 @@
         for p in range(10)
     ]
 
-    base = view * 8
-    first = [cam_ref[base + j] for j in range(4)]
-    second = [cam_ref[base + 4 + j] for j in range(4)]
+    first = [cam_ref[view, 0, j] for j in range(4)]
+    second = [cam_ref[view, 1, j] for j in range(4)]
     variance = [jnp.exp(2.0 * values[3 + j]) for j in range(3)]
     half = 0.5 * TILE_SIDE
     center_x = first[0] * values[0] + first[1] * values[1] + first[2] * values[2] + first[3] + half
@@ -207,6 +217,7 @@
         0, groups, forward, ([ones] * chunks, [zeros] * (3 * chunks)), unroll=2
     )
 
+    chosen = lax.broadcasted_iota(jnp.int32, (slabs, LANES), 0) == tile
     behinds = []
     for c in range(chunks):
         part = slice(c * LANES, (c + 1) * LANES)
@@ -221,7 +232,9 @@
             lit = run * color[3 * c + k]
             shade = jnp.sum(lit, axis=0, keepdims=True) + left * back_ref[k]
             image_ref[k : k + 1, part] = shade
-            miss = shade - target_ref[tile, k : k + 1, part]
+            miss = shade - jnp.sum(
+                jnp.where(chosen, target_ref[k, :, part], 0.0), axis=0, keepdims=True
+            )
             misses[k, :, part] = jnp.broadcast_to(miss, (8, LANES))
             total = total + miss * shade
             pulled = pulled + miss * lit
@@ -290,8 +303,8 @@
 
 
 def collect_kernel(
-    tiles, depths, own_ref, image_ref, lists_ref, out_ref, images_ref,
-    inbox, partial, pieces, mine,
+    tiles, depths, own_ref, image_ref, lists_ref, gradient_ref, picture_ref,
+    images_ref, out_ref, inbox, partial, pieces, mine,
     send, receive, image_send, image_recv, image_own, cut_send, cut_recv, all_send, all_recv,
 ):
     lines = out_ref.shape[0]
@@ -374,8 +387,15 @@
     for copy in shares:
         copy.start()
     out_ref[rows_of(me_d), :] = total
+    for d in range(depths):
+        for k in range(3):
+            picture_ref[k, d : d + 1, :] = images_ref[d, k : k + 1, :]
     for copy in shares:
         copy.wait()
+    for p in range(10):
+        for h in range(highs):
+            line = p * highs + h
+            gradient_ref[p : p + 1, h * LANES : (h + 1) * LANES] = out_ref[line : line + 1, :]
 
 
 def adam_update(param, first, second, gradient):
@@ -398,7 +418,6 @@
     params = jnp.concatenate([positions, log_scales, opacity_logits, colors], axis=0)
     splats = params.shape[1]
     lines = 10 * splats // LANES
-    named = jnp.stack([list_owner[0, :, :, 0], list_row[0]], axis=1)
     tile_count = lax.axis_size("tile")
     assert 10 * slab * depth_count % LANES == 0 and slab == LANES
     smem = pl.BlockSpec(memory_space=pltpu.SMEM)
@@ -412,9 +431,11 @@
             jax.ShapeDtypeStruct((tile_count, depth_count, 2, slab), jnp.int32),
             jax.ShapeDtypeStruct(block, F32),
         ],
-        in_specs=[vmem] * 2,
+        in_specs=[vmem] * 6,
         out_specs=[vmem] * 2,
         scratch_shapes=[
+            pltpu.VMEM((depth_count, 2, slab), jnp.int32),
+            pltpu.VMEM((lines, LANES), F32),
             pltpu.VMEM((lines, 2 * LANES), BF16),
             pltpu.VMEM((lines, LANES), BF16),
             pltpu.VMEM((tile_count,) + block, F32),
@@ -429,7 +450,10 @@
         compiler_params=pltpu.CompilerParams(
             collective_id=1, has_side_effects=True, vmem_limit_bytes=limit
         ),
-    )(named, params.reshape(lines, LANES))
+    )(
+        list_owner.reshape(tiles_here, 1, slab), list_row[0],
+        positions, log_scales, opacity_logits, colors,
+    )
     own_image, own_grad = pl.pallas_call(
         render_kernel,
         out_shape=[
@@ -448,17 +472,19 @@
         ],
         name="render",
         compiler_params=pltpu.CompilerParams(vmem_limit_bytes=limit),
-    )(here, tile_view, tile_length, cameras.reshape(-1), background, entry, target)
+    )(here, tile_view, tile_length, cameras, background, entry, target.transpose(1, 0, 2))
     quarter = lines // depth_count
-    total, image = pl.pallas_call(
+    gradient, picture = pl.pallas_call(
         functools.partial(collect_kernel, tile_count, depth_count),
         out_shape=[
-            jax.ShapeDtypeStruct((lines, LANES), F32),
-            jax.ShapeDtypeStruct((depth_count, 3, pixels), F32),
+            jax.ShapeDtypeStruct((10, splats), F32),
+            jax.ShapeDtypeStruct((3, depth_count, pixels), F32),
         ],
         in_specs=[vmem] * 3,
         out_specs=[vmem] * 2,
         scratch_shapes=[
+            pltpu.VMEM((depth_count, 3, pixels), F32),
+            pltpu.VMEM((lines, LANES), F32),
             pltpu.VMEM((tile_count,) + block, F32),
             pltpu.VMEM((lines, LANES), F32),
             pltpu.VMEM((depth_count, quarter, LANES), F32),
@@ -478,7 +504,7 @@
             collective_id=2, has_side_effects=True, vmem_limit_bytes=limit
         ),
     )(own_grad, own_image, lists)
-    gradient = total.reshape(10, splats)
+    image = picture.transpose(1, 0, 2)
     new_params, new_first, new_second = adam_update(params, first_moment, second_moment, gradient)
     return (image, new_params, new_first, new_second)
 

time: 55.8 us -> 50.8 us (0.910)
  local copies, waits for them, and re-layouts: 6.01 us -> 0.65 us
    unnamed x20 -> x13, local copies, waits for them, and re-layouts: 3.78 us -> 0.65 us
    reshape x3 -> x0, local copies, waits for them, and re-layouts: 2.22 us -> none  [the longest x1 0.94 us: body(): gradient = total.reshape(10, splats)]
    sub x1, other arithmetic: 0.83 us -> 1.81 us  [adam_update(): return (param - 0.05 * corrected, new_first, new_second)]
    another operation x1 -> x0, other arithmetic: 0.6 us -> none  [body(): named = jnp.stack([list_owner[0, :, :, 0], list_row[0]], axis=1)]
where the time goes in v3:
time: 50.8 us; the launch traced here: 50.5 us
  Pallas kernels  47.3 us (93%)
  other arithmetic  1.81 us (4%)
  between operations  0.72 us (1%)
  local copies, waits for them, and re-layouts  0.65 us (1%)
    pallas_call x1, Pallas kernels, body(): pl.pallas_call(functools.partial(fetch_kernel, tile_count, depth_count),...  18.3 us
    pallas_call x1, Pallas kernels, body(): pl.pallas_call(functools.partial(collect_kernel, tile_count, depth_count)...  16.9 us
    pallas_call x1, Pallas kernels, body(): pl.pallas_call(render_kernel, out_shape=[jax.ShapeDtypeStruct((3, pixels)...  12.2 us
    sub x1, other arithmetic, adam_update(): return (param - 0.05 * corrected, new_first, new_second)  1.81 us

profile of v3, /device:TPU:0, one launch (start us, length us, event | category | flops | bytes accessed | tf_op | source)
XLA Modules:
  0.0 50.5 jit_solution(16262434576973128273)
XLA Ops:
  0.6 0.0 copy-start.3
  0.6 18.3 %fetch.1 = (s32[8,4,2,128]{3,2,1,0:T(2,128)}, f32[40,128]{1,0:T(8,128)}) custom-call(s32[4,1,128]{2,1,0:T(1,128)} %bitcast.7, s32[4,128]{1,0:T(4,128)} %bitcast.8, f32[3,2048]{1,0:T(4,128)} %place_ref.1, f32[3,2048]{1,0:T(4,128)} %scale_ref.1, f32[1,2048]{1,0:T(1,128)} %logit_ref.1, f32[3,2048]{1,0:T(4,128)} %color_ref.1), custom_call_target="tpu_custom_call" | custom-call | tf_op jit(solution)/shard_map/fetch/pallas_call | solution.py:428
  18.9 0.0 copy-start.2
  18.9 12.2 %render.1 = (f32[3,1024]{1,0:T(4,128)}, f32[40,128]{1,0:T(8,128)}) custom-call(s32[1]{0:T(128)} %bitcast.where_ref, s32[4]{0:T(128)} %view_ref.1, s32[4]{0:T(128)} %length_ref.1, f32[4,2,4]{2,1,0:T(2,128)} %cam_ref.1, f32[3]{0:T(128)} %back_ref.1, f32[40,128]{1,0:T(8,128)} %get-tuple-element.10.entry_ref, f32[3,4,1024]{2,1,0:T(4,128)} %bitcast.5), custom_call_target="tpu_custom_call" | custom-call | tf_op jit(solution)/shard_map/render/pallas_call | solution.py:457
  31.1 0.0 copy-start
  31.1 0.0 copy-start.1
  31.1 0.0 copy-start.5
  31.1 16.9 %collect.1 = (f32[10,2048]{1,0:T(8,128)}, f32[3,4,1024]{2,1,0:T(4,128)}) custom-call(f32[40,128]{1,0:T(8,128)} %get-tuple-element.11.own_ref, f32[3,1024]{1,0:T(4,128)} %get-tuple-element.12.image_ref, s32[8,4,2,128]{3,2,1,0:T(2,128)} %get-tuple-element.13.lists_ref), custom_call_target="tpu_custom_call" | custom-call | tf_op jit(solution)/shard_map/collect/pallas_call | solution.py:477
  48.0 0.0 copy-done.3
  48.0 0.0 copy-done.2
  48.0 0.0 copy-done
  48.0 0.0 copy-done.1
  48.0 0.0 copy-done.5
  48.0 0.0 copy-start.4
  48.0 1.8 %maximum_subtract_fusion = (f32[10,2048]{1,0:T(8,128)}, f32[10,2048]{1,0:T(8,128)}, f32[10,2048]{1,0:T(8,128)}) fusion(f32[3,2048]{1,0:T(4,128)S(1)} %copy-done.2, f32[1,2048]{1,0:T(1,128)S(1)} %copy-done.5, f32[3,2048]{1,0:T(4,128)S(1)} %copy-done.1, f32[3,2048]{1,0:T(4,128)S(1)} %copy-done, f32[10,2048]{1,0:T(8,128)} %get-tuple-element.15, ...), kind=kLoop, calls=%fused_computation.2 | loop fusion | flops 327680 | bytes 573440 | tf_op jit(solution)/shard_map/sub | solution.py:405
  49.8 0.0 copy-done.4
  49.9 0.6 %copy.18 = f32[4,3,1024]{2,0,1:T(4,128)} copy(f32[4,3,1024]{2,0,1:T(4,128)S(1)} %bitcast.6) | data formatting | bytes 98304
Async XLA Ops:
  0.6 47.3 %copy-start.3 = (f32[10,2048]{1,0:T(8,128)S(1)}, f32[10,2048]{1,0:T(8,128)}, u32[]{:S(2)}) copy-start(f32[10,2048]{1,0:T(8,128)} %param.17) | copy-start | bytes 245764
  18.9 29.1 %copy-start.2 = (f32[3,2048]{1,0:T(4,128)S(1)}, f32[3,2048]{1,0:T(4,128)}, u32[]{:S(2)}) copy-start(f32[3,2048]{1,0:T(4,128)} %color_ref.1) | copy-start | bytes 73732
  31.1 16.9 %copy-start = (f32[3,2048]{1,0:T(4,128)S(1)}, f32[3,2048]{1,0:T(4,128)}, u32[]{:S(2)}) copy-start(f32[3,2048]{1,0:T(4,128)} %place_ref.1) | copy-start | bytes 73732
  31.1 16.9 %copy-start.1 = (f32[3,2048]{1,0:T(4,128)S(1)}, f32[3,2048]{1,0:T(4,128)}, u32[]{:S(2)}) copy-start(f32[3,2048]{1,0:T(4,128)} %scale_ref.1) | copy-start | bytes 73732
  31.1 16.9 %copy-start.5 = (f32[1,2048]{1,0:T(1,128)S(1)}, f32[1,2048]{1,0:T(1,128)}, u32[]{:S(2)}) copy-start(f32[1,2048]{1,0:T(1,128)} %logit_ref.1) | copy-start | bytes 24580
  48.0 1.8 %copy-start.4 = (f32[3,4,1024]{2,1,0:T(4,128)S(1)}, f32[3,4,1024]{2,1,0:T(4,128)}, u32[]{:S(2)}) copy-start(f32[3,4,1024]{2,1,0:T(4,128)} %get-tuple-element.14) | copy-start | bytes 147460

commit v4 on v3

--- a/solution.py
+++ b/solution.py
@@ -142,7 +142,7 @@
     where_ref, view_ref, length_ref, cam_ref, back_ref,
     entry_ref, target_ref,
     image_ref, grad_ref,
-    alphas, transes, misses, carries, columns, sums,
+    alphas, weights, misses, carries, columns, sums,
 ):
     slabs = target_ref.shape[1]
     slab = entry_ref.shape[1]
@@ -204,8 +204,8 @@
             t = trans[c]
             part = slice(c * LANES, (c + 1) * LANES)
             alphas[at, part] = alpha
-            transes[at, part] = t
             weight = alpha * t
+            weights[at, part] = weight
             new_trans.append(t - weight)
             new_color.append(color[3 * c] + weight * red)
             new_color.append(color[3 * c + 1] + weight * green)
@@ -214,7 +214,7 @@
 
     zeros = jnp.zeros((8, LANES), F32)
     trans, color = lax.fori_loop(
-        0, groups, forward, ([ones] * chunks, [zeros] * (3 * chunks)), unroll=2
+        0, groups, forward, ([ones] * chunks, [zeros] * (3 * chunks)), unroll=4
     )
 
     chosen = lax.broadcasted_iota(jnp.int32, (slabs, LANES), 0) == tile
@@ -255,9 +255,8 @@
         for c in range(chunks):
             part = slice(c * LANES, (c + 1) * LANES)
             alpha = alphas[at, part]
-            t = transes[at, part] * carries[:, part]
+            weight = weights[at, part] * carries[:, part]
             m0, m1, m2 = misses[0, :, part], misses[1, :, part], misses[2, :, part]
-            weight = alpha * t
             pull = m0 * red + m1 * green + m2 * blue
             rest = behind[c] - weight * pull
             new_behind.append(rest)
@@ -278,7 +277,7 @@
         sums[spaced, :] = packed
         return new_behind
 
-    lax.fori_loop(0, groups, backward, behinds, unroll=2)
+    lax.fori_loop(0, groups, backward, behinds, unroll=4)
 
     flat = sums[...].T
     s0, sx, sy, sxx, sxy, syy, d_red, d_green, d_blue = [flat[j : j + 1, :] for j in range(9)]

time: 50.8 us -> 47.2 us (0.929)
  Pallas kernels: 47.3 us -> 43.8 us
    pallas_call x1, Pallas kernels: 12.2 us -> 8.64 us  [body(): pl.pallas_call(render_kernel, out_shape=[jax.ShapeDtypeStruct((3, pixels)...]
where the time goes in v4:
time: 47.2 us; the launch traced here: 46.9 us
  Pallas kernels  43.8 us (93%)
  other arithmetic  1.81 us (4%)
  between operations  0.72 us (2%)
  local copies, waits for them, and re-layouts  0.65 us (1%)
    pallas_call x1, Pallas kernels, body(): pl.pallas_call(functools.partial(fetch_kernel, tile_count, depth_count),...  18.3 us
    pallas_call x1, Pallas kernels, body(): pl.pallas_call(functools.partial(collect_kernel, tile_count, depth_count)...  16.9 us
    pallas_call x1, Pallas kernels, body(): pl.pallas_call(render_kernel, out_shape=[jax.ShapeDtypeStruct((3, pixels)...  8.64 us
    sub x1, other arithmetic, adam_update(): return (param - 0.05 * corrected, new_first, new_second)  1.81 us

profile of v4, /device:TPU:0, one launch (start us, length us, event | category | flops | bytes accessed | tf_op | source)
XLA Modules:
  0.0 46.9 jit_solution(10150077368214545945)
XLA Ops:
  0.6 0.0 copy-start.3
  0.6 18.3 %fetch.1 = (s32[8,4,2,128]{3,2,1,0:T(2,128)}, f32[40,128]{1,0:T(8,128)}) custom-call(s32[4,1,128]{2,1,0:T(1,128)} %bitcast.7, s32[4,128]{1,0:T(4,128)} %bitcast.8, f32[3,2048]{1,0:T(4,128)} %place_ref.1, f32[3,2048]{1,0:T(4,128)} %scale_ref.1, f32[1,2048]{1,0:T(1,128)} %logit_ref.1, f32[3,2048]{1,0:T(4,128)} %color_ref.1), custom_call_target="tpu_custom_call" | custom-call | tf_op jit(solution)/shard_map/fetch/pallas_call | solution.py:427
  18.9 0.0 copy-start.2
  18.9 8.6 %render.1 = (f32[3,1024]{1,0:T(4,128)}, f32[40,128]{1,0:T(8,128)}) custom-call(s32[1]{0:T(128)} %bitcast.where_ref, s32[4]{0:T(128)} %view_ref.1, s32[4]{0:T(128)} %length_ref.1, f32[4,2,4]{2,1,0:T(2,128)} %cam_ref.1, f32[3]{0:T(128)} %back_ref.1, f32[40,128]{1,0:T(8,128)} %get-tuple-element.10.entry_ref, f32[3,4,1024]{2,1,0:T(4,128)} %bitcast.5), custom_call_target="tpu_custom_call" | custom-call | tf_op jit(solution)/shard_map/render/pallas_call | solution.py:456
  27.6 0.0 copy-start
  27.6 0.0 copy-start.1
  27.6 0.0 copy-start.5
  27.6 16.9 %collect.1 = (f32[10,2048]{1,0:T(8,128)}, f32[3,4,1024]{2,1,0:T(4,128)}) custom-call(f32[40,128]{1,0:T(8,128)} %get-tuple-element.11.own_ref, f32[3,1024]{1,0:T(4,128)} %get-tuple-element.12.image_ref, s32[8,4,2,128]{3,2,1,0:T(2,128)} %get-tuple-element.13.lists_ref), custom_call_target="tpu_custom_call" | custom-call | tf_op jit(solution)/shard_map/collect/pallas_call | solution.py:476
  44.5 0.0 copy-done.3
  44.5 0.0 copy-done.2
  44.5 0.0 copy-done
  44.5 0.0 copy-done.1
  44.5 0.0 copy-done.5
  44.5 0.0 copy-start.4
  44.5 1.8 %maximum_subtract_fusion = (f32[10,2048]{1,0:T(8,128)}, f32[10,2048]{1,0:T(8,128)}, f32[10,2048]{1,0:T(8,128)}) fusion(f32[3,2048]{1,0:T(4,128)S(1)} %copy-done.2, f32[1,2048]{1,0:T(1,128)S(1)} %copy-done.5, f32[3,2048]{1,0:T(4,128)S(1)} %copy-done.1, f32[3,2048]{1,0:T(4,128)S(1)} %copy-done, f32[10,2048]{1,0:T(8,128)} %get-tuple-element.15, ...), kind=kLoop, calls=%fused_computation.2 | loop fusion | flops 327680 | bytes 573440 | tf_op jit(solution)/shard_map/sub | solution.py:404
  46.3 0.0 copy-done.4
  46.3 0.6 %copy.18 = f32[4,3,1024]{2,0,1:T(4,128)} copy(f32[4,3,1024]{2,0,1:T(4,128)S(1)} %bitcast.6) | data formatting | bytes 98304
Async XLA Ops:
  0.6 43.8 %copy-start.3 = (f32[10,2048]{1,0:T(8,128)S(1)}, f32[10,2048]{1,0:T(8,128)}, u32[]{:S(2)}) copy-start(f32[10,2048]{1,0:T(8,128)} %param.17) | copy-start | bytes 245764
  18.9 25.5 %copy-start.2 = (f32[3,2048]{1,0:T(4,128)S(1)}, f32[3,2048]{1,0:T(4,128)}, u32[]{:S(2)}) copy-start(f32[3,2048]{1,0:T(4,128)} %color_ref.1) | copy-start | bytes 73732
  27.6 16.9 %copy-start = (f32[3,2048]{1,0:T(4,128)S(1)}, f32[3,2048]{1,0:T(4,128)}, u32[]{:S(2)}) copy-start(f32[3,2048]{1,0:T(4,128)} %place_ref.1) | copy-start | bytes 73732
  27.6 16.9 %copy-start.1 = (f32[3,2048]{1,0:T(4,128)S(1)}, f32[3,2048]{1,0:T(4,128)}, u32[]{:S(2)}) copy-start(f32[3,2048]{1,0:T(4,128)} %scale_ref.1) | copy-start | bytes 73732
  27.6 16.9 %copy-start.5 = (f32[1,2048]{1,0:T(1,128)S(1)}, f32[1,2048]{1,0:T(1,128)}, u32[]{:S(2)}) copy-start(f32[1,2048]{1,0:T(1,128)} %logit_ref.1) | copy-start | bytes 24580
  44.5 1.8 %copy-start.4 = (f32[3,4,1024]{2,1,0:T(4,128)S(1)}, f32[3,4,1024]{2,1,0:T(4,128)}, u32[]{:S(2)}) copy-start(f32[3,4,1024]{2,1,0:T(4,128)} %get-tuple-element.14) | copy-start | bytes 147460
